TPU v7x, 256 devices: a whole 4x4x8 slice. The times are simulated.
256 devices in a mesh: dp: 16 (over z, core), spatial: 16 (over x, y).
Axes of the slice: x: 4, y: 4, z: 8, core: 2. Of those that a mesh axis runs over, the one named last changes fastest.
Arguments:
- fields: bfloat16 [192, 1024, 768], P('spatial', 'dp'), may hold values from -6 to 6
- filter_weight: float32 [2, 1024, 192], P(None, 'dp'), may hold values from -8 to 8
- cotangent: bfloat16 [192, 1024, 768], P('spatial', 'dp'), may hold values from -6 to 6
Outputs:
- activated: bfloat16 [192, 1024, 768], P('spatial', 'dp')
- grad_fields: bfloat16 [192, 1024, 768], P('spatial', 'dp')
- grad_weight: float32 [2, 1024, 192], P(None, 'dp')
All inputs are finite; a program needn't handle non-finite values.
Results may differ from a plain program's by a relative error of at most 0.014.
Values may be sent and summed in bfloat16 or wider, within the bound.
A program may use at most 64 MiB of HBM per device.

v0:
```python
import functools
import math

import jax
import jax.numpy as jnp
import ml_dtypes
import numpy as np
from jax import lax
from jax.sharding import PartitionSpec as P


@functools.lru_cache(None)
def legendre_table(nlat):
    theta = np.pi * (np.arange(nlat) + 0.5) / nlat
    cosine, sine = np.cos(theta), np.sin(theta)
    table = np.zeros((nlat, nlat, nlat))
    diagonal = np.full((nlat,), 1.0 / math.sqrt(4.0 * math.pi))
    for m in range(nlat):
        if m:
            diagonal = -math.sqrt((2.0 * m + 1.0) / (2.0 * m)) * sine * diagonal
        table[m, m] = diagonal
        if m + 1 < nlat:
            table[m, m + 1] = math.sqrt(2.0 * m + 3.0) * cosine * diagonal
    orders = np.arange(nlat)
    for l in range(2, nlat):
        m = orders[: l - 1, None].astype(np.float64)
        scale = np.sqrt((4.0 * l * l - 1.0) / (l * l - m * m))
        last = np.sqrt((4.0 * (l - 1) ** 2 - 1.0) / ((l - 1) ** 2 - m * m))
        table[: l - 1, l] = scale * (cosine * table[: l - 1, l - 1] - table[: l - 1, l - 2] / last)
    return table


@functools.lru_cache(None)
def fourier_tables(nlon, modes):
    points, orders = np.arange(nlon)[:, None], np.arange(modes)[None, :]
    angle = 2.0 * np.pi / nlon * (points * orders % nlon)
    parts = np.stack([np.cos(angle), -np.sin(angle)], axis=1)
    factor = np.where(orders == 0, 1.0, 2.0)[:, None]
    forward = (2.0 * np.pi / nlon * parts).astype(ml_dtypes.bfloat16)
    inverse = (factor * parts).astype(ml_dtypes.bfloat16)
    return forward, inverse


def shards(fields, filter_weight, cotangent):
    lat_rows, width, nlon = fields.shape
    spatial = lax.axis_size("spatial")
    nlat = lat_rows * spatial
    me = lax.axis_index("spatial")
    f32, bf16 = jnp.float32, jnp.bfloat16
    forward, inverse = (
        jnp.asarray(t.transpose(0, 2, 1).reshape(nlon, 2 * nlat)) for t in fourier_tables(nlon, nlat)
    )
    tables = legendre_table(nlat).reshape(spatial, lat_rows, nlat, nlat).astype(ml_dtypes.bfloat16)
    table = lax.dynamic_index_in_dim(jnp.asarray(tables), me, 0, keepdims=False)
    quad_w = (np.pi / nlat * np.sin(np.pi * (np.arange(nlat) + 0.5) / nlat)).astype(np.float32)
    own_w = lax.dynamic_slice_in_dim(jnp.asarray(quad_w), me * lat_rows, lat_rows, 0)
    wr, wi = filter_weight[0][None], filter_weight[1][None]
    dot = functools.partial(jnp.einsum, preferred_element_type=f32)

    spectra = (dot("jcn,nk->kcj", fields, forward) * own_w).astype(bf16)
    split = lax.all_to_all(spectra, "spatial", split_axis=0, concat_axis=2, tiled=True)
    split = split.reshape(lat_rows, 2, width, nlat)
    coeffs = dot("mlj,mpcj->mpcl", table, split)
    real_c, imag_c = coeffs[:, 0], coeffs[:, 1]
    filtered = jnp.stack([wr * real_c - wi * imag_c, wr * imag_c + wi * real_c], axis=1)
    synth = dot("mlj,mpcl->mpcj", table, filtered.astype(bf16)).reshape(2 * lat_rows, width, nlat)
    rows = lax.all_to_all(synth.astype(bf16), "spatial", split_axis=2, concat_axis=0, tiled=True)
    pre = dot("kcj,nk->jcn", rows, inverse)
    cdf = 0.5 * (1.0 + lax.erf(pre / math.sqrt(2.0)))
    density = jnp.exp(-0.5 * pre * pre) / math.sqrt(2.0 * math.pi)
    activated = (pre * cdf).astype(bf16)
    dpre = (cotangent.astype(f32) * (cdf + pre * density)).astype(bf16)
    dsynth = dot("jcn,nk->kcj", dpre, inverse).astype(bf16)
    dsplit = lax.all_to_all(dsynth, "spatial", split_axis=0, concat_axis=2, tiled=True)
    dsplit = dsplit.reshape(lat_rows, 2, width, nlat)
    dfiltered = dot("mlj,mpcj->mpcl", table, dsplit)
    real_d, imag_d = dfiltered[:, 0], dfiltered[:, 1]
    grad_real = jnp.sum(real_d * real_c + imag_d * imag_c, axis=0)
    grad_imag = jnp.sum(imag_d * real_c - real_d * imag_c, axis=0)
    partial_grad = jnp.stack([grad_real, grad_imag], axis=0).astype(bf16)
    dcoeffs = jnp.stack([wr * real_d + wi * imag_d, wr * imag_d - wi * real_d], axis=1)
    dspectra = dot("mlj,mpcl->mpcj", table, dcoeffs.astype(bf16)) * quad_w
    dspectra = dspectra.reshape(2 * lat_rows, width, nlat).astype(bf16)
    drows = lax.all_to_all(dspectra, "spatial", split_axis=2, concat_axis=0, tiled=True)
    grad_fields = dot("kcj,nk->jcn", drows, forward).astype(bf16)

    pieces = partial_grad.reshape(2, spatial, width // spatial, nlat).transpose(1, 0, 2, 3)
    pieces = lax.all_to_all(pieces, "spatial", split_axis=0, concat_axis=0, tiled=True)
    owned = (jnp.sum(pieces.astype(f32), axis=0) / nlat).astype(bf16)
    owned = jnp.broadcast_to(owned[None], (spatial,) + owned.shape)
    whole = lax.all_to_all(owned, "spatial", split_axis=0, concat_axis=0, tiled=True)
    grad_weight = whole.transpose(1, 0, 2, 3).reshape(2, width, nlat).astype(f32)
    return activated, grad_fields, grad_weight


def solution(mesh):
    in_specs = (P("spatial", "dp", None), P(None, "dp", None), P("spatial", "dp", None))
    out_specs = (P("spatial", "dp", None), P("spatial", "dp", None), P(None, "dp", None))
    return jax.shard_map(shards, mesh=mesh, in_specs=in_specs, out_specs=out_specs, check_vma=False)
```

profile of v0, /device:TPU:160, one launch (start us, length us, event | category | flops | bytes accessed | tf_op | source)
XLA Modules:
  0.0 125.9 jit_solution(1332953682050059228)
XLA Ops:
  1.9 1.8 %fusion.13 = bf16[384,64,12]{0,1,2:T(8,128)(2,1)S(1)} fusion(bf16[768,384,1]{1,0,2:T(8,128)(2,1)} %constant.46, bf16[12,64,768]{2,1,0:T(8,128)(2,1)S(1)} %copy-done, f32[12]{0:T(128)S(1)} %dynamic_slice.7), kind=kOutput, calls=%fused_computation.21 | convolution fusion | flops 453574656 | bytes 2359344 | tf_op jit(solution)/shard_map/jcn,nk->kcj/dot_general | solution.py:60
  3.8 1.6 %copy.40 = bf16[384,64,12]{1,2,0:T(8,128)(2,1)S(1)} copy(bf16[384,64,12]{0,1,2:T(8,128)(2,1)S(1)} %fusion.13) | data formatting | bytes 1179648 | tf_op jit(solution)/shard_map/convert_element_type | solution.py:60
  5.4 1.6 %reshape.46 = bf16[16,2,9216]{2,1,0:T(2,128)(2,1)} reshape(bf16[384,12,64]{2,1,0:T(8,128)(2,1)S(1)} %bitcast.80) | data formatting | bytes 1179648
  7.1 7.0 %all-to-all-start = ((bf16[16,2,9216]{2,1,0:T(2,128)(2,1)}), bf16[16,2,9216]{2,1,0:T(2,128)(2,1)S(1)}, u32[]{:S(2)}, u32[]{:S(2)}) async-start(bf16[16,2,9216]{2,1,0:T(2,128)(2,1)} %reshape.46), calls=%async_computation | async-start | bytes 1179648 | tf_op jit(solution)/shard_map/all_to_all | solution.py:61
  14.1 0.9 slice_bitcast_fusion.1
  15.0 11.0 %all-to-all-done = bf16[16,2,9216]{2,1,0:T(2,128)(2,1)S(1)} async-done(((bf16[16,2,9216]{2,1,0:T(2,128)(2,1)}), bf16[16,2,9216]{2,1,0:T(2,128)(2,1)S(1)}, u32[]{:S(2)}, u32[]{:S(2)}) %all-to-all-start) | async-done | bytes 589856 | tf_op jit(solution)/shard_map/all_to_all | solution.py:61
  26.0 0.9 reshape.47
  27.2 1.8 %fusion.18 = f32[12,2,64,192]{3,2,1,0:T(8,128)S(1)} fusion(bf16[16,12,192,192]{3,2,1,0:T(8,128)(2,1)} %constant.42.clone, s32[]{:T(128)S(6)} %select_n.8, bf16[12,2,64,192]{2,1,0,3:T(2,128)(2,1)S(1)} %bitcast.90), kind=kOutput, calls=%fused_computation.26 | convolution fusion | flops 113246208 | bytes 2949124 | tf_op jit(solution)/shard_map/mlj,mpcj->mpcl/dot_general | solution.py:63
  29.3 1.7 %convolution_convert_fusion.1 = bf16[12,2,64,192]{3,2,1,0:T(8,128)(2,1)S(1)} fusion(bf16[16,12,192,192]{3,2,1,0:T(8,128)(2,1)} %constant.42.clone, s32[]{:T(128)S(6)} %select_n.8, bf16[12,1,64,192]{3,2,1,0:T(8,128)(2,1)S(1)} %get-tuple-element.11, bf16[12,1,64,192]{3,2,1,0:T(8,128)(2,1)S(1)} %get-tuple-element.10), kind=kOutput, calls=%fused_computation.17 | convolution fusion | flops 113836032 | bytes 2359300 | tf_op jit(solution)/shard_map/mlj,mpcl->mpcj/dot_general | solution.py:66
  31.0 1.6 %copy.44 = bf16[24,64,192]{1,0,2:T(8,128)(2,1)} copy(bf16[24,64,192]{2,1,0:T(8,128)(2,1)S(1)} %bitcast.93) | data formatting | bytes 1179648 | tf_op jit(solution)/shard_map/convert_element_type | solution.py:67
  32.6 2.5 %reshape.48 = bf16[16,2,9216]{2,1,0:T(2,128)(2,1)S(1)} reshape(bf16[192,24,64]{2,1,0:T(8,128)(2,1)} %bitcast.86) | data formatting | bytes 1179648
  35.1 14.7 %all_to_all.76 = bf16[16,2,9216]{2,1,0:T(2,128)(2,1)} all-to-all(bf16[16,2,9216]{2,1,0:T(2,128)(2,1)S(1)} %reshape.48), channel_id=1, replica_groups=mesh['dp'=16,'spatial'=16] {'spatial'}, dimensions={0} | all-to-all | bytes 1179648 | tf_op jit(solution)/shard_map/all_to_all | solution.py:67
  49.8 3.2 %reshape.49 = bf16[192,24,64]{2,1,0:T(8,128)(2,1)} reshape(bf16[16,2,9216]{2,1,0:T(2,128)(2,1)} %all_to_all.76) | data formatting | bytes 1179648
  53.0 1.6 %copy.45 = bf16[16,24,64,12]{2,1,0,3:T(8,128)(2,1)S(1)} copy(bf16[16,24,64,12]{2,1,3,0:T(8,128)(2,1)} %bitcast.84) | data formatting | bytes 1179648 | tf_op jit(solution)/shard_map/all_to_all | solution.py:67
  54.6 2.3 %fusion.9 = (bf16[12,64,768]{2,1,0:T(8,128)(2,1)}, f32[64,12,768]{2,0,1:T(8,128)S(1)}) fusion(bf16[384,64,12]{1,0,2:T(8,128)(2,1)S(1)} %bitcast.88, bf16[768,384,1]{1,0,2:T(8,128)(2,1)S(1)} %copy-done.6), kind=kOutput, calls=%fused_computation.12 | convolution fusion | flops 455933952 | bytes 4718592 | tf_op jit(solution)/shard_map/kcj,nk->jcn/dot_general | solution.py:68
  56.9 1.4 %fusion.12 = bf16[384,64,12]{0,1,2:T(8,128)(2,1)S(1)} fusion(bf16[768,384,1]{1,0,2:T(8,128)(2,1)S(1)} %copy-done.6, f32[64,12,768]{2,0,1:T(8,128)S(1)} %get-tuple-element.17, bf16[12,64,768]{2,1,0:T(8,128)(2,1)S(1)} %copy-done.7), kind=kOutput, calls=%fused_computation.20 | convolution fusion | flops 459767808 | bytes 4718592 | tf_op jit(solution)/shard_map/jcn,nk->kcj/dot_general | solution.py:73
  58.3 2.3 %copy.47 = bf16[384,64,12]{1,2,0:T(8,128)(2,1)} copy(bf16[384,64,12]{0,1,2:T(8,128)(2,1)S(1)} %fusion.12) | data formatting | bytes 1179648 | tf_op jit(solution)/shard_map/convert_element_type | solution.py:73
  60.6 2.1 %reshape.50 = bf16[16,2,9216]{2,1,0:T(2,128)(2,1)S(1)} reshape(bf16[384,12,64]{2,1,0:T(8,128)(2,1)} %bitcast.81) | data formatting | bytes 1179648
  62.6 13.8 %all_to_all.77 = bf16[16,2,9216]{2,1,0:T(2,128)(2,1)} all-to-all(bf16[16,2,9216]{2,1,0:T(2,128)(2,1)S(1)} %reshape.50), channel_id=1, replica_groups=mesh['dp'=16,'spatial'=16] {'spatial'}, dimensions={0} | all-to-all | bytes 1179648 | tf_op jit(solution)/shard_map/all_to_all | solution.py:74
  76.4 2.8 %reshape.51 = bf16[384,12,64]{2,1,0:T(8,128)(2,1)} reshape(bf16[16,2,9216]{2,1,0:T(2,128)(2,1)} %all_to_all.77) | data formatting | bytes 1179648
  79.3 1.7 %copy.49 = bf16[24,64,16,12]{1,0,3,2:T(8,128)(2,1)S(1)} copy(bf16[24,64,16,12]{1,3,0,2:T(8,128)(2,1)} %bitcast.83) | data formatting | bytes 1179648 | tf_op jit(solution)/shard_map/all_to_all | solution.py:74
  81.0 1.8 %fusion.15 = f32[12,2,64,192]{3,2,1,0:T(8,128)S(1)} fusion(bf16[16,12,192,192]{3,2,1,0:T(8,128)(2,1)} %constant.42.clone, s32[]{:T(128)S(6)} %select_n.8, bf16[12,2,64,192]{2,1,0,3:T(2,128)(2,1)S(1)} %bitcast.91), kind=kOutput, calls=%fused_computation.23 | convolution fusion | flops 113246208 | bytes 2949124 | tf_op jit(solution)/shard_map/mlj,mpcj->mpcl/dot_general | solution.py:76
  82.9 1.2 add_reduce_fusion
  84.2 10.9 %all_to_all.78 = bf16[16,2,4,192]{3,2,1,0:T(4,128)(2,1)S(1)} all-to-all(bf16[16,2,4,192]{3,2,1,0:T(4,128)(2,1)S(1)} %maximum_bitcast_fusion), channel_id=1, replica_groups=mesh['dp'=16,'spatial'=16] {'spatial'}, dimensions={0} | all-to-all | bytes 98304 | tf_op jit(solution)/shard_map/all_to_all | solution.py:88
  95.8 4.2 %all-to-all-start.5 = ((bf16[16,2,4,192]{3,2,1,0:T(4,128)(2,1)}), bf16[16,2,4,192]{3,2,1,0:T(4,128)(2,1)}, u32[]{:S(2)}, u32[]{:S(2)}) async-start(bf16[16,2,4,192]{3,2,1,0:T(4,128)(2,1)} %broadcast_in_dim.2), calls=%async_computation.5 | async-start | bytes 131072 | tf_op jit(solution)/shard_map/all_to_all | solution.py:91
  100.0 1.8 %multiply_convert_fusion = bf16[12,2,64,192]{3,2,1,0:T(8,128)(2,1)S(1)} fusion(bf16[16,12,192,192]{3,2,1,0:T(8,128)(2,1)} %constant.42.clone, s32[]{:T(128)S(6)} %select_n.8, bf16[12,1,64,192]{3,2,1,0:T(8,128)(2,1)S(1)} %get-tuple-element.12, bf16[12,1,64,192]{3,2,1,0:T(8,128)(2,1)} %get-tuple-element.13, f32[192]{0:T(256)S(1)} %copy-done.8), kind=kOutput, calls=%fused_computation.13 | convolution fusion | flops 114130944 | bytes 2458372 | tf_op jit(solution)/shard_map/mlj,mpcl->mpcj/dot_general | solution.py:82
  101.8 1.2 copy.51
  102.9 1.5 %reshape.52 = bf16[16,2,9216]{2,1,0:T(2,128)(2,1)} reshape(bf16[192,24,64]{2,1,0:T(8,128)(2,1)S(1)} %bitcast.87) | data formatting | bytes 1179648
  104.4 3.2 %all-to-all-done.5 = bf16[16,2,4,192]{3,2,1,0:T(4,128)(2,1)} async-done(((bf16[16,2,4,192]{3,2,1,0:T(4,128)(2,1)}), bf16[16,2,4,192]{3,2,1,0:T(4,128)(2,1)}, u32[]{:S(2)}, u32[]{:S(2)}) %all-to-all-start.5) | async-done | bytes 49184 | tf_op jit(solution)/shard_map/all_to_all | solution.py:91
  107.6 3.9 %all-to-all-start.3 = ((bf16[16,2,9216]{2,1,0:T(2,128)(2,1)}), bf16[16,2,9216]{2,1,0:T(2,128)(2,1)S(1)}, u32[]{:S(2)}, u32[]{:S(2)}) async-start(bf16[16,2,9216]{2,1,0:T(2,128)(2,1)} %reshape.52), calls=%async_computation.3 | async-start | bytes 1179648 | tf_op jit(solution)/shard_map/all_to_all | solution.py:84
  113.1 8.9 %all-to-all-done.3 = bf16[16,2,9216]{2,1,0:T(2,128)(2,1)S(1)} async-done(((bf16[16,2,9216]{2,1,0:T(2,128)(2,1)}), bf16[16,2,9216]{2,1,0:T(2,128)(2,1)S(1)}, u32[]{:S(2)}, u32[]{:S(2)}) %all-to-all-start.3) | async-done | bytes 589856 | tf_op jit(solution)/shard_map/all_to_all | solution.py:84
  123.7 2.2 %fusion.10 = bf16[12,64,768]{2,1,0:T(8,128)(2,1)} fusion(bf16[384,64,12]{1,0,2:T(8,128)(2,1)S(1)} %bitcast.89, bf16[768,384,1]{1,0,2:T(8,128)(2,1)S(1)} %copy-done.5), kind=kOutput, calls=%fused_computation.15 | convolution fusion | flops 453574656 | bytes 2359296 | tf_op jit(solution)/shard_map/kcj,nk->jcn/dot_general | solution.py:85
  (32 shorter events, 6.0 us)
Async XLA Ops:
  0.6 1.3 %copy-start = (bf16[12,64,768]{2,1,0:T(8,128)(2,1)S(1)}, bf16[12,64,768]{2,1,0:T(8,128)(2,1)}, u32[]{:S(2)}) copy-start(bf16[12,64,768]{2,1,0:T(8,128)(2,1)} %param.7) | copy-start | bytes 3538948
  7.1 18.9 %all-to-all-start = ((bf16[16,2,9216]{2,1,0:T(2,128)(2,1)}), bf16[16,2,9216]{2,1,0:T(2,128)(2,1)S(1)}, u32[]{:S(2)}, u32[]{:S(2)}) async-start(bf16[16,2,9216]{2,1,0:T(2,128)(2,1)} %reshape.46), calls=%async_computation | async-start | bytes 1179648 | tf_op jit(solution)/shard_map/all_to_all | solution.py:61
  15.0 14.1 %copy-start.1 = (f32[64,192]{1,0:T(8,128)}, f32[64,192]{1,0:T(8,128)S(1)}, u32[]{:S(2)}) copy-start(f32[64,192]{1,0:T(8,128)S(1)} %get-tuple-element.14) | copy-start | bytes 147460
  15.0 14.1 %copy-start.3 = (f32[64,192]{1,0:T(8,128)}, f32[64,192]{1,0:T(8,128)S(1)}, u32[]{:S(2)}) copy-start(f32[64,192]{1,0:T(8,128)S(1)} %get-tuple-element.15) | copy-start | bytes 147460
  53.0 1.6 %copy-start.6 = (bf16[768,384,1]{1,0,2:T(8,128)(2,1)S(1)}, bf16[768,384,1]{1,0,2:T(8,128)(2,1)}, u32[]{:S(2)}) copy-start(bf16[768,384,1]{1,0,2:T(8,128)(2,1)} %constant.47) | copy-start | bytes 1769476
  54.6 2.3 %copy-start.7 = (bf16[12,64,768]{2,1,0:T(8,128)(2,1)S(1)}, bf16[12,64,768]{2,1,0:T(8,128)(2,1)}, u32[]{:S(2)}) copy-start(bf16[12,64,768]{2,1,0:T(8,128)(2,1)} %param.9) | copy-start | bytes 3538948
  81.0 1.9 %copy-start.2 = (f32[64,192]{1,0:T(8,128)S(1)}, f32[64,192]{1,0:T(8,128)}, u32[]{:S(2)}) copy-start(f32[64,192]{1,0:T(8,128)} %copy-done.1) | copy-start | bytes 147460
  81.0 1.9 %copy-start.4 = (f32[64,192]{1,0:T(8,128)S(1)}, f32[64,192]{1,0:T(8,128)}, u32[]{:S(2)}) copy-start(f32[64,192]{1,0:T(8,128)} %copy-done.3) | copy-start | bytes 147460
  82.9 17.1 %copy-start.8 = (f32[192]{0:T(256)S(1)}, f32[192]{0:T(256)}, u32[]{:S(2)}) copy-start(f32[192]{0:T(256)} %constant.43.clone) | copy-start | bytes 2308
  95.8 11.8 %all-to-all-start.5 = ((bf16[16,2,4,192]{3,2,1,0:T(4,128)(2,1)}), bf16[16,2,4,192]{3,2,1,0:T(4,128)(2,1)}, u32[]{:S(2)}, u32[]{:S(2)}) async-start(bf16[16,2,4,192]{3,2,1,0:T(4,128)(2,1)} %broadcast_in_dim.2), calls=%async_computation.5 | async-start | bytes 131072 | tf_op jit(solution)/shard_map/all_to_all | solution.py:91
  107.6 14.4 %all-to-all-start.3 = ((bf16[16,2,9216]{2,1,0:T(2,128)(2,1)}), bf16[16,2,9216]{2,1,0:T(2,128)(2,1)S(1)}, u32[]{:S(2)}, u32[]{:S(2)}) async-start(bf16[16,2,9216]{2,1,0:T(2,128)(2,1)} %reshape.52), calls=%async_computation.3 | async-start | bytes 1179648 | tf_op jit(solution)/shard_map/all_to_all | solution.py:84
  122.6 1.1 copy-start.5
where the time goes:
time: 127 us; the launch traced here: 126 us
  blocking collectives  39.4 us (31%)
  local copies, waits for them, and re-layouts  30.2 us (24%)
  waiting for transfers between devices  23 us (18%)
  starting transfers between devices  15.1 us (12%)
  matrix products  14.8 us (12%)
  other arithmetic  2.4 us (2%)
    unnamed x27, local copies, waits for them, and re-layouts  17.1 us
    all_to_all x1, blocking collectives, shards(): lax.all_to_all(synth.astype(bf16), 'spatial', split_axis=2, concat_axis=0...  14.7 us
    all_to_all x1, blocking collectives, shards(): lax.all_to_all(dsynth, 'spatial', split_axis=0, concat_axis=2, tiled=True)  13.8 us
    all_to_all x1, waiting for transfers between devices, shards(): lax.all_to_all(spectra, 'spatial', split_axis=0, concat_axis=2, tiled=True)  11 us
    all_to_all x1, blocking collectives, shards(): lax.all_to_all(pieces, 'spatial', split_axis=0, concat_axis=0, tiled=True)  10.9 us
    all_to_all x1, waiting for transfers between devices, shards(): lax.all_to_all(dspectra, 'spatial', split_axis=2, concat_axis=0, tiled=True)  8.85 us
    all_to_all x1, starting transfers between devices, shards(): lax.all_to_all(spectra, 'spatial', split_axis=0, concat_axis=2, tiled=True)  7.03 us
    all_to_all x1, starting transfers between devices, shards(): lax.all_to_all(owned, 'spatial', split_axis=0, concat_axis=0, tiled=True)  4.15 us
  transfers between devices with their start and end apart: 3, of which 3 were waited for; matrix products, arithmetic and copies ran while one was open for 5% of the time, Pallas kernels for 0%

commit v1 on v0

v1 whole, which is shorter than its diff:
```python
import functools
import math

import jax
import jax.numpy as jnp
import ml_dtypes
import numpy as np
from jax import lax
from jax.experimental import pallas as pl
from jax.experimental.pallas import tpu as pltpu
from jax.sharding import PartitionSpec as P

MESH = pl.DeviceIdType.MESH
F32, BF16 = jnp.float32, jnp.bfloat16

N = 16
ROWS = 12
WIDTH = 64
NLAT = N * ROWS
NLON = 768
GROUPS, TILES = 3, 3
FULL = N * GROUPS * TILES
REST = N * GROUPS
BLOCK = GROUPS * TILES * 16


@functools.lru_cache(None)
def constants():
    f32, bf16 = np.float32, ml_dtypes.bfloat16
    full = [ROWS * d + 4 * g + t for d in range(N) for g in range(GROUPS) for t in range(TILES)]
    rest = [ROWS * d + 4 * g + 3 for d in range(N) for g in range(GROUPS)]
    orders = np.array(full + rest)
    angle = 2.0 * np.pi / NLON * (orders[:, None] * np.arange(NLON)[None, :] % NLON)
    parts = np.concatenate([np.cos(angle), -np.sin(angle)], axis=0)
    factor = np.where(orders == 0, 1.0, 2.0)[:, None]
    forward = (2.0 * np.pi / NLON * parts).astype(bf16)
    inverse = (np.concatenate([factor, factor], axis=0) * parts).astype(bf16)

    theta = np.pi * (np.arange(NLAT) + 0.5) / NLAT
    cosine, sine = np.cos(theta), np.sin(theta)
    weights = np.pi / NLAT * sine
    row_weights = np.zeros((N, 16, 128), f32)
    row_weights[:, :ROWS] = weights.reshape(N, ROWS, 1)

    lane = np.arange(256)
    s, r = lane // 16, lane % 16
    own = r < ROWS
    rows_of = [np.where(own, ROWS * s + r, ROWS * s + 4 * t + r - ROWS) for t in range(TILES)]
    col_weights = np.stack([np.repeat(weights[j][:, None], 128, 1) for j in rows_of]).astype(f32)

    diagonal = np.zeros((NLAT, NLAT))
    diagonal[0] = 1.0 / math.sqrt(4.0 * math.pi)
    for m in range(1, NLAT):
        diagonal[m] = -math.sqrt((2.0 * m + 1.0) / (2.0 * m)) * sine * diagonal[m - 1]
    m, l = np.arange(NLAT)[:, None].astype(float), np.arange(NLAT)[None, :].astype(float)
    above = l > m
    scale = np.where(above, np.sqrt(np.where(above, 4 * l * l - 1, 1.0) / np.where(above, l * l - m * m, 1.0)), 0.0)
    last = l - 1
    two = last > m
    scale_last = np.sqrt(np.where(two, 4 * last * last - 1, 1.0) / np.where(two, last * last - m * m, 1.0))
    back = np.where(two, scale / scale_last, 0.0)

    cos_map = np.zeros((16, 256), f32)
    order_map = np.full((16, 256), -1.0, f32)
    diag_map = np.zeros((N, 16, 256), f32)
    coef = np.zeros((N, 64, 256), f32)
    for g in range(GROUPS):
        for t in range(TILES):
            v = TILES * g + t
            cos_map[v] = cosine[rows_of[t]]
            order_map[v] = np.where(own, 4 * g + t, 4 * g + 3)
            for d in range(N):
                ma, mb = ROWS * d + 4 * g + t, ROWS * d + 4 * g + 3
                diag_map[d, v] = np.where(own, diagonal[ma][rows_of[t]], diagonal[mb][rows_of[t]])
                for kind, values in enumerate((scale[ma], scale[mb], back[ma], back[mb])):
                    coef[d, 16 * kind + v, :NLAT] = values
    maps = np.concatenate([cos_map, order_map], axis=0)
    return dict(
        forward=forward, inverse=inverse, row_weights=row_weights, col_weights=col_weights,
        maps=maps, diag=diag_map, coef=coef,
    )


def kernel(
    x_hbm, cot_hbm, weight_hbm, ft_hbm, gt_hbm, roww_hbm, colw_hbm, maps_hbm, diag_hbm, coef_hbm,
    act_hbm, gf_hbm, gw_hbm,
    xv, cotv, weightv, ftv, gtv, rowwv, colwv, mapsv, diagv, coefv,
    stage, send, recv, legendre0, legendre1, table, table_t, coeffs, rotated, prev, tt, actv, dprev,
    gsend, grecv, gout, gall, sums, gwv,
    load_sem, store_sem, send_a, recv_a, send_g, recv_g, send_r, recv_r,
):
    dp, me = lax.axis_index("dp"), lax.axis_index("spatial")
    peer_of = lambda s: lax.rem(me + s, N)

    loads = [
        pltpu.make_async_copy(src, dst, load_sem.at[i])
        for i, (src, dst) in enumerate((
            (x_hbm, xv), (ft_hbm, ftv), (roww_hbm.at[me], rowwv), (coef_hbm.at[me], coefv),
            (diag_hbm.at[me], diagv), (maps_hbm, mapsv), (weight_hbm, weightv), (gt_hbm, gtv),
            (cot_hbm, cotv), (colw_hbm, colwv),
        ))
    ]
    for load in loads:
        load.start()

    barrier = pltpu.get_barrier_semaphore()

    def greet(s, _):
        pl.semaphore_signal(barrier, inc=1, device_id=(dp, peer_of(s)), device_id_type=MESH)
        return 0

    lax.fori_loop(1, N, greet, 0)

    low = lax.broadcasted_iota(jnp.int32, (1, 128), 1) < WIDTH
    half = lambda value: pltpu.roll(value, WIDTH, 1)

    def whole_copy(phase, peer):
        return pltpu.make_async_remote_copy(
            src_ref=send.at[phase, peer], dst_ref=recv.at[phase, me],
            send_sem=send_a.at[phase, peer], recv_sem=recv_a.at[phase, me],
            device_id=(dp, peer), device_id_type=MESH,
        )

    def whole_arrival(phase, src):
        return pltpu.make_async_remote_copy(
            src_ref=recv.at[phase, src], dst_ref=recv.at[phase, src],
            send_sem=send_a.at[phase, src], recv_sem=recv_a.at[phase, src],
            device_id=(dp, src), device_id_type=MESH,
        )

    def group_rows(g):
        return pl.ds(pl.multiple_of(g * 48, 48), 48)

    def group_copy(phase, g, peer):
        return pltpu.make_async_remote_copy(
            src_ref=send.at[phase, peer, group_rows(g)], dst_ref=recv.at[phase, me, group_rows(g)],
            send_sem=send_g.at[phase // 2, g, peer], recv_sem=recv_g.at[phase // 2, g, me],
            device_id=(dp, peer), device_id_type=MESH,
        )

    def group_arrival(phase, g, src):
        ref = recv.at[phase, src, group_rows(g)]
        return pltpu.make_async_remote_copy(
            src_ref=ref, dst_ref=ref,
            send_sem=send_g.at[phase // 2, g, src], recv_sem=recv_g.at[phase // 2, g, src],
            device_id=(dp, src), device_id_type=MESH,
        )

    def fourier(q, rows_ref, factors, scaled):
        block = rows_ref[pl.ds(pl.multiple_of(q * 256, 256), 256), :]
        out = lax.dot_general(factors[...], block, (((1,), (1,)), ((), ())), preferred_element_type=F32)
        for u in range(2):
            real, imag = out[:NLAT, 128 * u : 128 * u + 128], out[NLAT:, 128 * u : 128 * u + 128]
            pair = (jnp.where(low, real, half(imag)), jnp.where(low, half(real), imag))
            for i, value in enumerate(pair):
                j = 4 * q + 2 * u + i
                if scaled:
                    value = value * rowwv[pl.ds(j, 1), :]
                stage[pl.ds(j, FULL, stride=16), :] = value[:FULL]
                stage[pl.ds(q * 16 + ROWS + 2 * u + i, REST, stride=48), :] = value[FULL:]
        return 0

    def ship(phase):
        recv[phase, me] = stage[pl.ds(pl.multiple_of(me * BLOCK, BLOCK), BLOCK), :].astype(BF16)

        def one(s, _):
            peer = peer_of(s)
            send[phase, peer] = stage[pl.ds(pl.multiple_of(peer * BLOCK, BLOCK), BLOCK), :].astype(BF16)
            whole_copy(phase, peer).start()
            return 0

        lax.fori_loop(1, N, one, 0)

    def each_peer(action):
        def one(s, _):
            action(peer_of(s))
            return 0

        lax.fori_loop(1, N, one, 0)

    for load in loads[:3]:
        load.wait()
    lax.fori_loop(0, 3, lambda q, _: fourier(q, xv, ftv, True), 0)
    pl.semaphore_wait(barrier, N - 1)
    ship(0)

    for load in loads[3:]:
        load.wait()
    own_lane = lax.broadcasted_iota(jnp.int32, (1, 128), 1) % 16 < ROWS
    first = (ROWS * me).astype(F32)

    for h in range(2):
        def degrees(g, carry, h=h):
            shift = lax.rem(128 - 8 * g, 128)
            turned = pltpu.roll(coefv[:, 128 * h : 128 * h + 128], shift, 1)
            for i in range(8):
                l = 128 * h + 8 * g + i
                pick = lambda kind: jnp.broadcast_to(turned[16 * kind : 16 * kind + 16, i : i + 1], (16, 128))
                scale = jnp.where(own_lane, pick(0), pick(1))
                back = jnp.where(own_lane, pick(2), pick(3))
                new = []
                for u, store in ((0, legendre0), (1, legendre1)):
                    cols = slice(128 * u, 128 * u + 128)
                    last, before = carry[2 * u], carry[2 * u + 1]
                    start = jnp.where(mapsv[16:, cols] + first == l.astype(F32), diagv[:, cols], 0.0)
                    value = (scale * mapsv[:16, cols]) * last + (start - back * before)
                    store[pl.ds(l, 16, stride=NLAT), :] = value
                    new += [value, last]
                carry = tuple(new)
            return carry

        if h == 0:
            carry = (jnp.zeros((16, 128), F32),) * 4
        carry = lax.fori_loop(0, 16 if h == 0 else 8, degrees, carry)

    def finish(v, _):
        rows = pl.ds(pl.multiple_of(v * NLAT, NLAT), NLAT)
        for u, store in ((0, legendre0), (1, legendre1)):
            part = store[rows, :].astype(BF16)
            table[v, :, 128 * u : 128 * u + 128] = part
            table_t[v, 128 * u : 128 * u + 128, :] = part.T
        return 0

    lax.fori_loop(0, GROUPS * TILES, finish, 0)

    weights = weightv[...].T
    filt = jnp.where(low, weights, half(weights))
    rotated[0] = filt
    filt = jnp.where(low, -half(weights), weights)
    rotated[1] = filt

    own_row = lax.broadcasted_iota(jnp.int32, (256, 128), 0) % 16 < ROWS

    def analyse(phase, g):
        found, fourth = [], None
        for t in range(TILES):
            rows = pl.ds(pl.multiple_of((TILES * g + t) * 16, 16), 16)
            block = recv[phase, :, rows, :].reshape(256, 128)
            zero = jnp.zeros_like(block)
            both = jnp.concatenate([jnp.where(own_row, block, zero), jnp.where(own_row, zero, block)], axis=1)
            out = jnp.dot(table[TILES * g + t], both, preferred_element_type=F32)
            found.append(out[:, :128])
            fourth = out[:, 128:] if fourth is None else fourth + out[:, 128:]
        return found + [fourth]

    def synthesize(phase, g, values, scaled):
        for t in range(TILES):
            both = jnp.concatenate([values[t], values[3]], axis=1)
            out = jnp.dot(table_t[TILES * g + t], both, preferred_element_type=F32)
            out = jnp.where(own_row, out[:, :128], out[:, 128:])
            if scaled:
                out = out * colwv[t]
            rows = pl.ds(pl.multiple_of((TILES * g + t) * 16, 16), 16)
            send[phase, :, rows, :] = out.astype(BF16).reshape(N, 16, 128)
        each_peer(lambda peer: group_copy(phase, g, peer).start())
        recv[phase, me, group_rows(g), :] = send[phase, me, group_rows(g), :]

    each_peer(lambda src: whole_arrival(0, src).wait_recv())

    def forward_group(g, _):
        values = []
        for i, value in enumerate(analyse(0, g)):
            coeffs[4 * g + i] = value
            values.append((rotated[0] * value + rotated[1] * half(value)).astype(BF16))
        synthesize(1, g, values, False)
        return 0

    lax.fori_loop(0, GROUPS, forward_group, 0)

    def gather(phase):
        def one(s, _):
            src = peer_of(s)

            @pl.when(s > 0)
            def _():
                for g in range(GROUPS):
                    group_arrival(phase, g, src).wait_recv()

            stage[pl.ds(pl.multiple_of(src * BLOCK, BLOCK), BLOCK), :] = recv[phase, src].astype(F32)
            return 0

        lax.fori_loop(0, N, one, 0)

        def spread(j, _):
            full = stage[pl.ds(j, FULL, stride=16), :]
            rest = stage[pl.ds((j // 4) * 16 + ROWS + lax.rem(j, 4), REST, stride=48), :]
            turned = jnp.concatenate([full, rest], axis=0).astype(BF16).T
            rows = pl.ds(pl.multiple_of(j * WIDTH, WIDTH), WIDTH)
            tt[0, rows, :] = turned[:WIDTH]
            tt[1, rows, :] = turned[WIDTH:]
            return 0

        lax.fori_loop(0, ROWS, spread, 0)

    def grid_rows(q, factors):
        rows = pl.ds(pl.multiple_of(q * 256, 256), 256)
        return jnp.dot(tt[0, rows, :], factors[:NLAT, :], preferred_element_type=F32) + jnp.dot(
            tt[1, rows, :], factors[NLAT:, :], preferred_element_type=F32
        )

    gather(1)

    def activation(q, _):
        prev[...] = grid_rows(q, gtv)

        def strip(i, _):
            here = pl.ds(pl.multiple_of(i * 16, 16), 16)
            there = pl.ds(pl.multiple_of(q * 256 + i * 16, 16), 16)
            pre = prev[here, :]
            cdf = 0.5 + 0.5 * lax.erf(pre * (1.0 / math.sqrt(2.0)))
            density = jnp.exp(-0.5 * pre * pre) * (1.0 / math.sqrt(2.0 * math.pi))
            actv[there, :] = (pre * cdf).astype(BF16)
            dprev[there, :] = (cotv[there, :].astype(F32) * (cdf + pre * density)).astype(BF16)
            return 0

        lax.fori_loop(0, 16, strip, 0)
        return fourier(q, dprev, gtv, False)

    lax.fori_loop(0, 3, activation, 0)
    ship(2)
    act_store = pltpu.make_async_copy(actv, act_hbm, store_sem.at[0])
    act_store.start()

    sums[...] = jnp.zeros_like(sums)
    each_peer(lambda src: whole_arrival(2, src).wait_recv())

    def backward_group(g, _):
        values = []
        for i, value in enumerate(analyse(2, g)):
            coeff, turned = coeffs[4 * g + i], half(value)
            sums[0] = sums[0] + value * coeff
            sums[1] = sums[1] + value * half(coeff)
            values.append((rotated[0] * value - rotated[1] * turned).astype(BF16))
        synthesize(3, g, values, True)
        return 0

    lax.fori_loop(0, GROUPS, backward_group, 0)

    same, cross = sums[0], sums[1]
    partial = jnp.where(low, same + half(same), cross - half(cross)).astype(BF16)
    gsend[:ROWS] = partial.reshape(ROWS, 16, 128)
    gsend[ROWS:] = jnp.zeros((N - ROWS, 16, 128), BF16)

    def sum_copy(peer):
        return pltpu.make_async_remote_copy(
            src_ref=gsend.at[peer], dst_ref=grecv.at[me], send_sem=send_r.at[0, peer], recv_sem=recv_r.at[0, me],
            device_id=(dp, peer), device_id_type=MESH,
        )

    def sum_arrival(src):
        return pltpu.make_async_remote_copy(
            src_ref=grecv.at[src], dst_ref=grecv.at[src], send_sem=send_r.at[0, src], recv_sem=recv_r.at[0, src],
            device_id=(dp, src), device_id_type=MESH,
        )

    def all_copy(peer):
        return pltpu.make_async_remote_copy(
            src_ref=gout, dst_ref=gall.at[me], send_sem=send_r.at[1, peer], recv_sem=recv_r.at[1, me],
            device_id=(dp, peer), device_id_type=MESH,
        )

    def all_arrival(src):
        return pltpu.make_async_remote_copy(
            src_ref=gall.at[src], dst_ref=gall.at[src], send_sem=send_r.at[1, src], recv_sem=recv_r.at[1, src],
            device_id=(dp, src), device_id_type=MESH,
        )

    each_peer(lambda peer: sum_copy(peer).start())
    grecv[me] = gsend[me]
    each_peer(lambda src: sum_arrival(src).wait_recv())
    total = jnp.sum(grecv[...].astype(F32), axis=0) * (1.0 / NLAT)
    gout[...] = total.astype(BF16)
    gall[me] = total.astype(BF16)
    each_peer(lambda peer: all_copy(peer).start())

    gather(3)

    def gradient(q, _):
        rows = pl.ds(pl.multiple_of(q * 256, 256), 256)
        xv[rows, :] = grid_rows(q, ftv).astype(BF16)
        pltpu.make_async_copy(xv.at[rows], gf_hbm.at[rows], store_sem.at[2 + q]).start()
        return 0

    lax.fori_loop(0, 3, gradient, 0)

    each_peer(lambda src: all_arrival(src).wait_recv())
    gwv[...] = gall[:ROWS].reshape(NLAT, 128).astype(F32).T
    gw_store = pltpu.make_async_copy(gwv, gw_hbm, store_sem.at[1])
    gw_store.start()

    def drain(s, _):
        peer = peer_of(s)
        for phase in (0, 2):
            whole_copy(phase, peer).wait_send()
        for phase in (1, 3):
            for g in range(GROUPS):
                group_copy(phase, g, peer).wait_send()
        sum_copy(peer).wait_send()
        all_copy(peer).wait_send()
        return 0

    lax.fori_loop(1, N, drain, 0)
    act_store.wait()
    gw_store.wait()
    for q in range(3):
        rows = pl.ds(q * 256, 256)
        pltpu.make_async_copy(xv.at[rows], gf_hbm.at[rows], store_sem.at[2 + q]).wait()


def shards(fields, filter_weight, cotangent):
    rows, width, nlon = fields.shape
    if (rows, width, nlon) != (ROWS, WIDTH, NLON) or lax.axis_size("spatial") != N:
        raise ValueError("unexpected sizes")
    held = constants()
    names = ("forward", "inverse", "row_weights", "col_weights", "maps", "diag", "coef")
    flat = rows * width
    dma, vmem = pltpu.SemaphoreType.DMA, pltpu.VMEM
    activated, grad_fields, grad_weight = pl.pallas_call(
        kernel,
        out_shape=(
            jax.ShapeDtypeStruct((flat, nlon), BF16),
            jax.ShapeDtypeStruct((flat, nlon), BF16),
            jax.ShapeDtypeStruct((2 * width, NLAT), F32),
        ),
        in_specs=[pl.BlockSpec(memory_space=pl.ANY)] * 10,
        out_specs=(pl.BlockSpec(memory_space=pl.ANY),) * 3,
        scratch_shapes=[
            vmem((flat, nlon), BF16), vmem((flat, nlon), BF16), vmem((2 * width, NLAT), F32),
            vmem((2 * NLAT, nlon), BF16), vmem((2 * NLAT, nlon), BF16), vmem((16, 128), F32),
            vmem((TILES, 256, 128), F32), vmem((32, 256), F32), vmem((16, 256), F32), vmem((64, 256), F32),
            vmem((N * BLOCK, 128), F32), vmem((4, N, BLOCK, 128), BF16), vmem((4, N, BLOCK, 128), BF16),
            vmem((16 * NLAT, 128), F32), vmem((16 * NLAT, 128), F32),
            vmem((GROUPS * TILES, NLAT, 256), BF16), vmem((GROUPS * TILES, 256, NLAT), BF16),
            vmem((ROWS, NLAT, 128), F32), vmem((2, NLAT, 128), F32), vmem((256, nlon), F32),
            vmem((2, flat, NLAT), BF16), vmem((flat, nlon), BF16), vmem((flat, nlon), BF16),
            vmem((N, 16, 128), BF16), vmem((N, 16, 128), BF16), vmem((16, 128), BF16), vmem((N, 16, 128), BF16),
            vmem((2, NLAT, 128), F32), vmem((2 * width, NLAT), F32),
            dma((10,)), dma((5,)), dma((4, N)), dma((4, N)), dma((2, GROUPS, N)), dma((2, GROUPS, N)),
            dma((2, N)), dma((2, N)),
        ],
        compiler_params=pltpu.CompilerParams(
            collective_id=0, has_side_effects=True, vmem_limit_bytes=56 << 20
        ),
    )(
        fields.reshape(flat, nlon), cotangent.reshape(flat, nlon), filter_weight.reshape(2 * width, NLAT),
        *(jnp.asarray(held[name]) for name in names),
    )
    return (
        activated.reshape(rows, width, nlon), grad_fields.reshape(rows, width, nlon),
        grad_weight.reshape(2, width, NLAT),
    )


def solution(mesh):
    in_specs = (P("spatial", "dp", None), P(None, "dp", None), P("spatial", "dp", None))
    out_specs = (P("spatial", "dp", None), P("spatial", "dp", None), P(None, "dp", None))
    return jax.shard_map(shards, mesh=mesh, in_specs=in_specs, out_specs=out_specs, check_vma=False)
```

time: 127 us -> 65.2 us (0.51)
  Pallas kernels: 0 us -> 60.2 us
  blocking collectives: 39.4 us -> 0 us
  local copies, waits for them, and re-layouts: 30.2 us -> 4.14 us
  waiting for transfers between devices: 23 us -> 0 us
  starting transfers between devices: 15.1 us -> 0 us
  matrix products: 14.8 us -> 0 us
  other arithmetic: 2.4 us -> 0 us
    pallas_call x0 -> x1, Pallas kernels: none -> 60.2 us  [shards(): pl.pallas_call(kernel, out_shape=(jax.ShapeDtypeStruct((flat, nlon), BF16...]
    all_to_all x3 -> x0, blocking collectives: 39.4 us -> none  [the longest x1 14.7 us: shards(): lax.all_to_all(synth.astype(bf16), 'spatial', split_axis=2, concat_axis=0...]
    all_to_all x3 -> x0, waiting for transfers between devices: 23 us -> none  [the longest x1 11 us: shards(): lax.all_to_all(spectra, 'spatial', split_axis=0, concat_axis=2, tiled=True)]
    all_to_all x3 -> x0, starting transfers between devices: 15.1 us -> none  [the longest x1 7.03 us: shards(): lax.all_to_all(spectra, 'spatial', split_axis=0, concat_axis=2, tiled=True)]
    dot_general x8 -> x0, matrix products: 14.8 us -> none  [the longest x1 2.29 us: shards(): pre = dot('kcj,nk->jcn', rows, inverse)]
    unnamed x27 -> x7, local copies, waits for them, and re-layouts: 17.1 us -> 4.14 us
    convert_element_type x5 -> x0, local copies, waits for them, and re-layouts: 6.81 us -> none  [the longest x1 2.29 us: shards(): dsynth = dot('jcn,nk->kcj', dpre, inverse).astype(bf16)]
    all_to_all x4 -> x0, local copies, waits for them, and re-layouts: 3.89 us -> none  [the longest x1 1.71 us: shards(): lax.all_to_all(dsynth, 'spatial', split_axis=0, concat_axis=2, tiled=True)]
  transfers between devices with their start and end apart: 3 -> 0, of which waited for: 3 -> 0; matrix products, arithmetic and copies ran while one was open for 5% -> 0% of each run, Pallas kernels for 0% -> 0%
where the time goes in v1:
time: 65.2 us; the launch traced here: 65 us
  Pallas kernels  60.2 us (92%)
  local copies, waits for them, and re-layouts  4.14 us (6%)
    pallas_call x1, Pallas kernels, shards(): pl.pallas_call(kernel, out_shape=(jax.ShapeDtypeStruct((flat, nlon), BF16...  60.2 us
    unnamed x7, local copies, waits for them, and re-layouts  4.14 us

profile of v1, /device:TPU:160, one launch (start us, length us, event | category | flops | bytes accessed | tf_op | source)
XLA Modules:
  0.0 65.0 jit_solution(13267664871932717307)
XLA Ops:
  0.6 60.2 %shard_map.121 = (bf16[768,768]{1,0:T(8,128)(2,1)}, bf16[768,768]{1,0:T(8,128)(2,1)}, f32[128,192]{1,0:T(8,128)}) custom-call(bf16[768,768]{1,0:T(8,128)(2,1)} %bitcast.8, bf16[768,768]{1,0:T(8,128)(2,1)} %bitcast.9, f32[128,192]{1,0:T(8,128)} %bitcast.10, bf16[384,768]{1,0:T(8,128)(2,1)} %constant.14.clone.ft_hbm, bf16[384,768]{1,0:T(8,128)(2,1)} %constant.15.clone.gt_hbm, ...), custom_call_target="tpu_custom_call" | custom-call | tf_op jit(solution)/shard_map/pallas_call | solution.py:418
  60.9 0.0 copy-start
  60.9 2.5 %copy.16 = bf16[12,64,768]{2,1,0:T(8,128)(2,1)} copy(bf16[12,64,768]{2,1,0:T(8,128)(2,1)} %bitcast.7) | data formatting | bytes 2359296
  63.3 0.0 copy-done
  63.3 0.0 copy-start.1
  63.3 1.0 %copy.17 = bf16[12,64,768]{2,1,0:T(8,128)(2,1)} copy(bf16[12,64,768]{2,1,0:T(8,128)(2,1)S(1)} %bitcast.6) | data formatting | bytes 2359296
  64.4 0.0 copy-done.1
  64.4 0.7 %copy.18 = f32[2,64,192]{2,1,0:T(8,128)} copy(f32[2,64,192]{2,1,0:T(8,128)S(1)} %bitcast.11) | data formatting | bytes 196608
Async XLA Ops:
  60.9 2.5 %copy-start = (bf16[768,768]{1,0:T(8,128)(2,1)S(1)}, bf16[768,768]{1,0:T(8,128)(2,1)}, u32[]{:S(2)}) copy-start(bf16[768,768]{1,0:T(8,128)(2,1)} %get-tuple-element.7) | copy-start | bytes 3538948
  63.3 1.0 %copy-start.1 = (f32[128,192]{1,0:T(8,128)S(1)}, f32[128,192]{1,0:T(8,128)}, u32[]{:S(2)}) copy-start(f32[128,192]{1,0:T(8,128)} %get-tuple-element.8) | copy-start | bytes 294916

commit v2 on v0

v2 whole, which is shorter than its diff:
```python
import functools
import math

import jax
import jax.numpy as jnp
import ml_dtypes
import numpy as np
from jax import lax
from jax.experimental import pallas as pl
from jax.experimental.pallas import tpu as pltpu
from jax.sharding import PartitionSpec as P

MESH = pl.DeviceIdType.MESH
F32, BF16 = jnp.float32, jnp.bfloat16

N = 16
ROWS = 12
WIDTH = 64
NLAT = N * ROWS
NLON = 768
Q = 3
GROUPS = 3
PART = 48
OFFSETS = sorted(
    (divmod(s, 4) for s in range(1, N)), key=lambda o: -min(o[0], 4 - o[0]) - min(o[1], 4 - o[1])
)


@functools.lru_cache(None)
def constants():
    f32, bf16 = np.float32, ml_dtypes.bfloat16
    orders = np.arange(NLAT)
    angle = 2.0 * np.pi / NLON * (orders[:, None] * np.arange(NLON)[None, :] % NLON)
    parts = np.concatenate([np.cos(angle), -np.sin(angle)], axis=0)
    factor = np.where(orders == 0, 1.0, 2.0)[:, None]
    forward = (2.0 * np.pi / NLON * parts).astype(bf16)
    inverse = (np.concatenate([factor, factor], axis=0) * parts).astype(bf16)

    theta = np.pi * (np.arange(NLAT) + 0.5) / NLAT
    cosine, sine = np.cos(theta), np.sin(theta)
    weights = np.pi / NLAT * sine
    row_weights = np.zeros((N, 16, 128), f32)
    row_weights[:, :ROWS] = weights.reshape(N, ROWS, 1)

    lane = np.arange(256)
    s, i, r = lane // 16, lane % 16 // 4, lane % 4
    rows_of = [ROWS * s + 4 * q + r for q in range(Q)]
    col_weights = np.stack([np.repeat(weights[j][:, None], 128, 1) for j in rows_of]).astype(f32)

    diagonal = np.zeros((NLAT, NLAT))
    diagonal[0] = 1.0 / math.sqrt(4.0 * math.pi)
    for m in range(1, NLAT):
        diagonal[m] = -math.sqrt((2.0 * m + 1.0) / (2.0 * m)) * sine * diagonal[m - 1]
    m, l = np.arange(NLAT)[:, None].astype(float), np.arange(NLAT)[None, :].astype(float)
    above = l > m
    scale = np.sqrt(np.where(above, 4 * l * l - 1, 0.0) / np.where(above, l * l - m * m, 1.0))
    last = l - 1
    two = last > m
    scale_last = np.sqrt(np.where(two, 4 * last * last - 1, 1.0) / np.where(two, last * last - m * m, 1.0))
    back = np.where(two, scale / scale_last, 0.0)

    cos_map = np.zeros((16, 256), f32)
    order_map = np.full((16, 256), -1.0, f32)
    diag_map = np.zeros((N, 16, 256), f32)
    coef = np.zeros((N, 64, 256), f32)
    for q in range(Q):
        for g in range(GROUPS):
            cos_map[4 * q + g] = cosine[rows_of[q]]
            order_map[4 * q + g] = 4 * g + i
            for d in range(N):
                diag_map[d, 4 * q + g] = diagonal[ROWS * d + 4 * g + i, rows_of[q]]
    for g in range(GROUPS):
        for k in range(4):
            for d in range(N):
                for kind, values in enumerate((scale, back)):
                    for copy in range(2):
                        coef[d, 32 * kind + 8 * k + 4 * copy + g, :NLAT] = values[ROWS * d + 4 * g + k]
    maps = np.concatenate([cos_map, order_map], axis=0)
    return dict(
        forward=forward, inverse=inverse, row_weights=row_weights, col_weights=col_weights,
        maps=maps, diag=diag_map, coef=coef,
    )


def kernel(
    x_hbm, cot_hbm, weight_hbm, ft_hbm, gt_hbm, roww_hbm, colw_hbm, maps_hbm, diag_hbm, coef_hbm,
    act_hbm, gf_hbm, gw_hbm,
    xv, cotv, weightv, ftv, gtv, rowwv, colwv, mapsv, diagv, coefv,
    stage, send, recv, legendre0, legendre1, table, table_t, coeffs, dcoeffs, filtered, rotated, prev, tt, actv,
    dprev, gsend, grecv, gout, gall, sums, gwv,
    load_sem, store_sem, send_a, recv_a, send_r, recv_r,
):
    dp, me = lax.axis_index("dp"), lax.axis_index("spatial")
    mx, my = me // 4, lax.rem(me, 4)
    at = lambda dx, dy: lax.rem(mx + dx, 4) * 4 + lax.rem(my + dy, 4)
    peer_of = lambda s: lax.rem(me + s, N)

    def each_peer(action):
        def one(s, _):
            action(peer_of(s))
            return 0

        lax.fori_loop(1, N, one, 0)

    barrier = pltpu.get_barrier_semaphore()
    for dx, dy in OFFSETS:
        pl.semaphore_signal(barrier, inc=1, device_id=(dp, at(dx, dy)), device_id_type=MESH)

    quad = lambda q: pl.ds(pl.multiple_of(q * 256, 256), 256)

    def x_load(q):
        return pltpu.make_async_copy(x_hbm.at[quad(q)], xv.at[quad(q)], load_sem.at[q])

    loads = [
        pltpu.make_async_copy(src, dst, load_sem.at[3 + i])
        for i, (src, dst) in enumerate((
            (ft_hbm, ftv), (roww_hbm.at[me], rowwv), (coef_hbm.at[me], coefv),
            (diag_hbm.at[me], diagv), (maps_hbm, mapsv), (weight_hbm, weightv), (gt_hbm, gtv),
            (cot_hbm, cotv), (colw_hbm, colwv),
        ))
    ]
    loads[0].start()
    x_load(0).start()
    loads[1].start()
    x_load(1).start()
    x_load(2).start()
    for load in loads[2:]:
        load.start()

    low = lax.broadcasted_iota(jnp.int32, (1, 128), 1) < WIDTH
    half = lambda value: pltpu.roll(value, WIDTH, 1)

    def outgoing(phase, q, peer):
        return pltpu.make_async_remote_copy(
            src_ref=send.at[phase, q, peer], dst_ref=recv.at[phase, q, me],
            send_sem=send_a.at[phase, q, peer], recv_sem=recv_a.at[phase, q, me],
            device_id=(dp, peer), device_id_type=MESH,
        )

    def arrivals(phase, q):
        def arrival(src):
            ref = recv.at[phase, q, src]
            pltpu.make_async_remote_copy(
                src_ref=ref, dst_ref=ref, send_sem=send_a.at[phase, q, src], recv_sem=recv_a.at[phase, q, src],
                device_id=(dp, src), device_id_type=MESH,
            ).wait_recv()

        each_peer(arrival)

    def ship(phase, q):
        for dx, dy in OFFSETS:
            outgoing(phase, q, at(dx, dy)).start()
        recv[phase, q, me] = send[phase, q, me]

    def fourier(phase, q, rows_ref, factors, scaled):
        block = rows_ref[quad(q), :]
        out = lax.dot_general(factors[...], block, (((1,), (1,)), ((), ())), preferred_element_type=F32)
        for u in range(2):
            real, imag = out[:NLAT, 128 * u : 128 * u + 128], out[NLAT:, 128 * u : 128 * u + 128]
            pair = (jnp.where(low, real, half(imag)), jnp.where(low, half(real), imag))
            for i, value in enumerate(pair):
                r = 2 * u + i
                if scaled:
                    value = value * rowwv[pl.ds(4 * q + r, 1), :]
                stage[pl.ds(r, NLAT, stride=4), :] = value
        send[phase, q] = stage[...].astype(BF16).reshape(N, PART, 128)

    loads[0].wait()
    loads[1].wait()
    x_load(0).wait()
    fourier(0, 0, xv, ftv, True)
    pl.semaphore_wait(barrier, N - 1)
    ship(0, 0)

    def spectra(q, _):
        x_load(q).wait()
        fourier(0, q, xv, ftv, True)
        ship(0, q)
        return 0

    lax.fori_loop(1, Q, spectra, 0)

    for load in loads[2:]:
        load.wait()
    order_of_lane = lax.broadcasted_iota(jnp.int32, (1, 128), 1) % 16 // 4
    first = (ROWS * me).astype(F32)

    for h in range(2):
        def degrees(g, carry, h=h):
            turned = pltpu.roll(coefv[:, 128 * h : 128 * h + 128], lax.rem(128 - 8 * g, 128), 1)
            for i in range(8):
                l = 128 * h + 8 * g + i
                pick = lambda k: jnp.broadcast_to(turned[8 * k : 8 * k + 8, i : i + 1], (8, 128))
                choose = lambda k: jnp.where(
                    order_of_lane < 2,
                    jnp.where(order_of_lane == 0, pick(k), pick(k + 1)),
                    jnp.where(order_of_lane == 2, pick(k + 2), pick(k + 3)),
                )
                scale, back = choose(0), choose(4)
                scale, back = jnp.concatenate([scale, scale], axis=0), jnp.concatenate([back, back], axis=0)
                new = []
                for u, store in ((0, legendre0), (1, legendre1)):
                    cols = slice(128 * u, 128 * u + 128)
                    last, before = carry[2 * u], carry[2 * u + 1]
                    start = jnp.where(mapsv[16:, cols] + first == l.astype(F32), diagv[:, cols], 0.0)
                    value = (scale * mapsv[:16, cols]) * last + (start - back * before)
                    store[pl.ds(l, 16, stride=NLAT), :] = value
                    new += [value, last]
                carry = tuple(new)
            return carry

        if h == 0:
            carry = (jnp.zeros((16, 128), F32),) * 4
        carry = lax.fori_loop(0, 16 if h == 0 else 8, degrees, carry)

    def finish(v, _):
        rows = pl.ds(pl.multiple_of((4 * (v // GROUPS) + lax.rem(v, GROUPS)) * NLAT, NLAT), NLAT)
        for u, store in ((0, legendre0), (1, legendre1)):
            part = store[rows, :].astype(BF16)
            table[v, :, 128 * u : 128 * u + 128] = part
            table_t[v, 128 * u : 128 * u + 128, :] = part.T
        return 0

    lax.fori_loop(0, Q * GROUPS, finish, 0)

    weights = weightv[...].T
    rotated[0] = jnp.where(low, weights, half(weights))
    rotated[1] = jnp.where(low, -half(weights), weights)
    coeffs[...] = jnp.zeros_like(coeffs)
    dcoeffs[...] = jnp.zeros_like(dcoeffs)
    sums[...] = jnp.zeros_like(sums)

    order_of_row = lax.broadcasted_iota(jnp.int32, (256, 128), 0) % 16 // 4
    upper = lax.broadcasted_iota(jnp.int32, (1, 8, 128), 1) < 4
    tile = lambda g: pl.ds(pl.multiple_of(g * 16, 16), 16)

    def analyse(phase, q, into):
        arrivals(phase, q)

        def one(g, _):
            block = recv[phase, q, :, tile(g), :].reshape(256, 128)
            zero = jnp.zeros_like(block)
            spread = jnp.concatenate([jnp.where(order_of_row == k, block, zero) for k in range(4)], axis=1)
            into[g] = into[g] + jnp.dot(table[GROUPS * q + g], spread, preferred_element_type=F32)
            return 0

        lax.fori_loop(0, GROUPS, one, 0)
        return 0

    def synthesize(phase, q, scaled):
        def one(g, _):
            out = jnp.dot(table_t[GROUPS * q + g], filtered[g], preferred_element_type=F32)
            parts = [out[:, 128 * k : 128 * k + 128].reshape(N, 2, 8, 128) for k in range(4)]
            first_half = jnp.where(upper, parts[0][:, 0], parts[1][:, 0])
            second_half = jnp.where(upper, parts[2][:, 1], parts[3][:, 1])
            out = jnp.concatenate([first_half, second_half], axis=1)
            if scaled:
                out = out * colwv[q].reshape(N, 16, 128)
            send[phase, q, :, tile(g), :] = out.astype(BF16)
            return 0

        lax.fori_loop(0, GROUPS, one, 0)
        ship(phase, q)
        return 0

    lax.fori_loop(0, Q, lambda q, _: analyse(0, q, coeffs), 0)

    def filter_group(g, _):
        for k in range(4):
            cols = slice(128 * k, 128 * k + 128)
            value = coeffs[g, :, cols]
            filtered[g, :, cols] = (rotated[0] * value + rotated[1] * half(value)).astype(BF16)
        return 0

    lax.fori_loop(0, GROUPS, filter_group, 0)
    lax.fori_loop(0, Q, lambda q, _: synthesize(1, q, False), 0)

    def gather(phase, q):
        arrivals(phase, q)
        stage[...] = recv[phase, q].reshape(N * PART, 128).astype(F32)
        for r in range(4):
            turned = stage[pl.ds(r, NLAT, stride=4), :].astype(BF16).T
            tt[0, WIDTH * r : WIDTH * r + WIDTH, :] = turned[:WIDTH]
            tt[1, WIDTH * r : WIDTH * r + WIDTH, :] = turned[WIDTH:]

    def grid_rows(factors):
        return jnp.dot(tt[0], factors[:NLAT, :], preferred_element_type=F32) + jnp.dot(
            tt[1], factors[NLAT:, :], preferred_element_type=F32
        )

    def act_store(q):
        return pltpu.make_async_copy(actv.at[quad(q)], act_hbm.at[quad(q)], store_sem.at[q])

    def activation(q, _):
        gather(1, q)
        prev[...] = grid_rows(gtv)

        def strip(i, _):
            here = pl.ds(pl.multiple_of(i * 16, 16), 16)
            there = pl.ds(pl.multiple_of(q * 256 + i * 16, 16), 16)
            pre = prev[here, :]
            cdf = 0.5 + 0.5 * lax.erf(pre * (1.0 / math.sqrt(2.0)))
            density = jnp.exp(-0.5 * pre * pre) * (1.0 / math.sqrt(2.0 * math.pi))
            actv[there, :] = (pre * cdf).astype(BF16)
            dprev[there, :] = (cotv[there, :].astype(F32) * (cdf + pre * density)).astype(BF16)
            return 0

        lax.fori_loop(0, 16, strip, 0)
        fourier(2, q, dprev, gtv, False)
        ship(2, q)
        act_store(q).start()
        return 0

    lax.fori_loop(0, Q, activation, 0)

    lax.fori_loop(0, Q, lambda q, _: analyse(2, q, dcoeffs), 0)

    def adjoint_group(g, _):
        for k in range(4):
            cols = slice(128 * k, 128 * k + 128)
            value = dcoeffs[g, :, cols]
            filtered[g, :, cols] = (rotated[0] * value - rotated[1] * half(value)).astype(BF16)
        return 0

    lax.fori_loop(0, GROUPS, adjoint_group, 0)
    synthesize(3, 0, True)

    def sum_group(g, _):
        for k in range(4):
            cols = slice(128 * k, 128 * k + 128)
            value, coeff = dcoeffs[g, :, cols], coeffs[g, :, cols]
            sums[0] = sums[0] + value * coeff
            sums[1] = sums[1] + value * half(coeff)
        return 0

    lax.fori_loop(0, GROUPS, sum_group, 0)
    same, cross = sums[0], sums[1]
    partial = jnp.where(low, same + half(same), cross - half(cross)).astype(BF16)
    gsend[:ROWS] = partial.reshape(ROWS, 16, 128)
    gsend[ROWS:] = jnp.zeros((N - ROWS, 16, 128), BF16)

    def small_copy(turn, peer):
        return pltpu.make_async_remote_copy(
            src_ref=gout if turn else gsend.at[peer], dst_ref=(gall if turn else grecv).at[me],
            send_sem=send_r.at[turn, peer], recv_sem=recv_r.at[turn, me],
            device_id=(dp, peer), device_id_type=MESH,
        )

    def small_arrivals(turn):
        def arrival(src):
            ref = (gall if turn else grecv).at[src]
            pltpu.make_async_remote_copy(
                src_ref=ref, dst_ref=ref, send_sem=send_r.at[turn, src], recv_sem=recv_r.at[turn, src],
                device_id=(dp, src), device_id_type=MESH,
            ).wait_recv()

        each_peer(arrival)

    each_peer(lambda peer: small_copy(0, peer).start())
    grecv[me] = gsend[me]
    lax.fori_loop(1, Q, lambda q, _: synthesize(3, q, True), 0)

    small_arrivals(0)
    total = (jnp.sum(grecv[...].astype(F32), axis=0) * (1.0 / NLAT)).astype(BF16)
    gout[...] = total
    gall[me] = total
    each_peer(lambda peer: small_copy(1, peer).start())

    def gf_store(q):
        return pltpu.make_async_copy(xv.at[quad(q)], gf_hbm.at[quad(q)], store_sem.at[3 + q])

    def gradient(q, _):
        gather(3, q)
        xv[quad(q), :] = grid_rows(ftv).astype(BF16)
        gf_store(q).start()
        return 0

    lax.fori_loop(0, Q, gradient, 0)

    small_arrivals(1)
    gwv[...] = gall[:ROWS].reshape(NLAT, 128).astype(F32).T
    gw_store = pltpu.make_async_copy(gwv, gw_hbm, store_sem.at[6])
    gw_store.start()

    def drain(s, _):
        peer = peer_of(s)
        for phase in range(4):
            for q in range(Q):
                outgoing(phase, q, peer).wait_send()
        for turn in range(2):
            small_copy(turn, peer).wait_send()
        return 0

    lax.fori_loop(1, N, drain, 0)
    for q in range(Q):
        act_store(q).wait()
        gf_store(q).wait()
    gw_store.wait()


def hand_over(*refs):
    count = (len(refs) - 1) // 2
    copies = [pltpu.make_async_copy(refs[i], refs[count + i], refs[-1].at[i]) for i in range(count)]
    for copy in copies:
        copy.start()
    for copy in copies:
        copy.wait()


def shards(fields, filter_weight, cotangent):
    rows, width, nlon = fields.shape
    if (rows, width, nlon) != (ROWS, WIDTH, NLON) or lax.axis_size("spatial") != N:
        raise ValueError("unexpected sizes")
    held = constants()
    names = ("forward", "inverse", "row_weights", "col_weights", "maps", "diag", "coef")
    flat = rows * width
    dma, vmem = pltpu.SemaphoreType.DMA, pltpu.VMEM
    shapes = (
        jax.ShapeDtypeStruct((flat, nlon), BF16),
        jax.ShapeDtypeStruct((flat, nlon), BF16),
        jax.ShapeDtypeStruct((2 * width, NLAT), F32),
    )
    results = pl.pallas_call(
        kernel,
        out_shape=shapes,
        in_specs=[pl.BlockSpec(memory_space=pl.ANY)] * 10,
        out_specs=(pl.BlockSpec(memory_space=pl.ANY),) * 3,
        scratch_shapes=[
            vmem((flat, nlon), BF16), vmem((flat, nlon), BF16), vmem((2 * width, NLAT), F32),
            vmem((2 * NLAT, nlon), BF16), vmem((2 * NLAT, nlon), BF16), vmem((16, 128), F32),
            vmem((Q, 256, 128), F32), vmem((32, 256), F32), vmem((16, 256), F32), vmem((64, 256), F32),
            vmem((N * PART, 128), F32), vmem((4, Q, N, PART, 128), BF16), vmem((4, Q, N, PART, 128), BF16),
            vmem((16 * NLAT, 128), F32), vmem((16 * NLAT, 128), F32),
            vmem((Q * GROUPS, NLAT, 256), BF16), vmem((Q * GROUPS, 256, NLAT), BF16),
            vmem((GROUPS, NLAT, 512), F32), vmem((GROUPS, NLAT, 512), F32), vmem((GROUPS, NLAT, 512), BF16),
            vmem((2, NLAT, 128), F32), vmem((256, nlon), F32),
            vmem((2, 256, NLAT), BF16), vmem((flat, nlon), BF16), vmem((flat, nlon), BF16),
            vmem((N, 16, 128), BF16), vmem((N, 16, 128), BF16), vmem((16, 128), BF16), vmem((N, 16, 128), BF16),
            vmem((2, NLAT, 128), F32), vmem((2 * width, NLAT), F32),
            dma((12,)), dma((7,)), dma((4, Q, N)), dma((4, Q, N)), dma((2, N)), dma((2, N)),
        ],
        compiler_params=pltpu.CompilerParams(
            collective_id=0, has_side_effects=True, vmem_limit_bytes=56 << 20
        ),
    )(
        fields.reshape(flat, nlon), cotangent.reshape(flat, nlon), filter_weight.reshape(2 * width, NLAT),
        *(jnp.asarray(held[name]) for name in names),
    )
    activated, grad_fields, grad_weight = pl.pallas_call(
        hand_over,
        out_shape=shapes,
        in_specs=[pl.BlockSpec(memory_space=pl.ANY)] * 3,
        out_specs=(pl.BlockSpec(memory_space=pl.ANY),) * 3,
        scratch_shapes=[dma((3,))],
    )(*results)
    return (
        activated.reshape(rows, width, nlon), grad_fields.reshape(rows, width, nlon),
        grad_weight.reshape(2, width, NLAT),
    )


def solution(mesh):
    in_specs = (P("spatial", "dp", None), P(None, "dp", None), P("spatial", "dp", None))
    out_specs = (P("spatial", "dp", None), P("spatial", "dp", None), P(None, "dp", None))
    return jax.shard_map(shards, mesh=mesh, in_specs=in_specs, out_specs=out_specs, check_vma=False)
```

time: 127 us -> 131 us (1.031)
  Pallas kernels: 0 us -> 130 us
  blocking collectives: 39.4 us -> 0 us
  local copies, waits for them, and re-layouts: 30.2 us -> 0 us
  waiting for transfers between devices: 23 us -> 0 us
  starting transfers between devices: 15.1 us -> 0 us
  matrix products: 14.8 us -> 0 us
  other arithmetic: 2.4 us -> 0 us
    pallas_call x0 -> x2, Pallas kernels: none -> 130 us  [the longest x1 76.6 us: shards(): pl.pallas_call(hand_over, out_shape=shapes, in_specs=[pl.BlockSpec(memory...]
    all_to_all x3 -> x0, blocking collectives: 39.4 us -> none  [the longest x1 14.7 us: shards(): lax.all_to_all(synth.astype(bf16), 'spatial', split_axis=2, concat_axis=0...]
    all_to_all x3 -> x0, waiting for transfers between devices: 23 us -> none  [the longest x1 11 us: shards(): lax.all_to_all(spectra, 'spatial', split_axis=0, concat_axis=2, tiled=True)]
    unnamed x27 -> x0, local copies, waits for them, and re-layouts: 17.1 us -> none
    all_to_all x3 -> x0, starting transfers between devices: 15.1 us -> none  [the longest x1 7.03 us: shards(): lax.all_to_all(spectra, 'spatial', split_axis=0, concat_axis=2, tiled=True)]
    dot_general x8 -> x0, matrix products: 14.8 us -> none  [the longest x1 2.29 us: shards(): pre = dot('kcj,nk->jcn', rows, inverse)]
    convert_element_type x5 -> x0, local copies, waits for them, and re-layouts: 6.81 us -> none  [the longest x1 2.29 us: shards(): dsynth = dot('jcn,nk->kcj', dpre, inverse).astype(bf16)]
    all_to_all x4 -> x0, local copies, waits for them, and re-layouts: 3.89 us -> none  [the longest x1 1.71 us: shards(): lax.all_to_all(dsynth, 'spatial', split_axis=0, concat_axis=2, tiled=True)]
  transfers between devices with their start and end apart: 3 -> 0, of which waited for: 3 -> 0; matrix products, arithmetic and copies ran while one was open for 5% -> 0% of each run, Pallas kernels for 0% -> 0%
where the time goes in v2:
time: 131 us
  Pallas kernels  130 us (99%)
    pallas_call x1, Pallas kernels, shards(): pl.pallas_call(hand_over, out_shape=shapes, in_specs=[pl.BlockSpec(memory...  76.6 us
    pallas_call x1, Pallas kernels, shards(): pl.pallas_call(kernel, out_shape=shapes, in_specs=[pl.BlockSpec(memory_sp...  53.5 us

profile of v2, /device:TPU:160, one launch (start us, length us, event | category | flops | bytes accessed | tf_op | source)
XLA Modules:
  0.0 130.7 jit_solution(4426273125040275938)
XLA Ops:
  0.6 53.5 %shard_map.121 = (bf16[768,768]{1,0:T(8,128)(2,1)}, bf16[768,768]{1,0:T(8,128)(2,1)}, f32[128,192]{1,0:T(8,128)}) custom-call(bf16[768,768]{1,0:T(8,128)(2,1)} %bitcast.6, bf16[768,768]{1,0:T(8,128)(2,1)} %bitcast.7, f32[128,192]{1,0:T(8,128)} %bitcast.8, bf16[384,768]{1,0:T(8,128)(2,1)} %constant.14.clone.ft_hbm, bf16[384,768]{1,0:T(8,128)(2,1)} %constant.15.clone.gt_hbm, ...), custom_call_target="tpu_custom_call" | custom-call | tf_op jit(solution)/shard_map/pallas_call | solution.py:423
  54.1 76.6 %shard_map.122 = (bf16[768,768]{1,0:T(8,128)(2,1)}, bf16[768,768]{1,0:T(8,128)(2,1)}, f32[128,192]{1,0:T(8,128)}) custom-call(bf16[768,768]{1,0:T(8,128)(2,1)} %get-tuple-element.9.refs_0_, bf16[768,768]{1,0:T(8,128)(2,1)} %get-tuple-element.10.refs_1_, f32[128,192]{1,0:T(8,128)} %get-tuple-element.11.refs_2_), custom_call_target="tpu_custom_call" | custom-call | tf_op jit(solution)/shard_map/pallas_call | solution.py:449

commit v3 on v2

--- a/solution.py
+++ b/solution.py
@@ -124,7 +124,7 @@
     loads[1].start()
     x_load(1).start()
     x_load(2).start()
-    for load in loads[2:]:
+    for load in loads[2:5]:
         load.start()
 
     low = lax.broadcasted_iota(jnp.int32, (1, 128), 1) < WIDTH
@@ -133,19 +133,16 @@
     def outgoing(phase, q, peer):
         return pltpu.make_async_remote_copy(
             src_ref=send.at[phase, q, peer], dst_ref=recv.at[phase, q, me],
-            send_sem=send_a.at[phase, q, peer], recv_sem=recv_a.at[phase, q, me],
+            send_sem=send_a.at[phase, q], recv_sem=recv_a.at[phase, q],
             device_id=(dp, peer), device_id_type=MESH,
         )
 
-    def arrivals(phase, q):
-        def arrival(src):
-            ref = recv.at[phase, q, src]
-            pltpu.make_async_remote_copy(
-                src_ref=ref, dst_ref=ref, send_sem=send_a.at[phase, q, src], recv_sem=recv_a.at[phase, q, src],
-                device_id=(dp, src), device_id_type=MESH,
-            ).wait_recv()
-
-        each_peer(arrival)
+    def whole(phase, q):
+        return pltpu.make_async_remote_copy(
+            src_ref=send.at[phase, q, pl.ds(0, N - 1)], dst_ref=recv.at[phase, q, pl.ds(0, N - 1)],
+            send_sem=send_a.at[phase, q], recv_sem=recv_a.at[phase, q],
+            device_id=(dp, peer_of(1)), device_id_type=MESH,
+        )
 
     def ship(phase, q):
         for dx, dy in OFFSETS:
@@ -171,6 +168,8 @@
     fourier(0, 0, xv, ftv, True)
     pl.semaphore_wait(barrier, N - 1)
     ship(0, 0)
+    for load in loads[5:]:
+        load.start()
 
     def spectra(q, _):
         x_load(q).wait()
@@ -180,16 +179,16 @@
 
     lax.fori_loop(1, Q, spectra, 0)
 
-    for load in loads[2:]:
+    for load in loads[2:5]:
         load.wait()
     order_of_lane = lax.broadcasted_iota(jnp.int32, (1, 128), 1) % 16 // 4
     first = (ROWS * me).astype(F32)
 
     for h in range(2):
         def degrees(g, carry, h=h):
-            turned = pltpu.roll(coefv[:, 128 * h : 128 * h + 128], lax.rem(128 - 8 * g, 128), 1)
-            for i in range(8):
-                l = 128 * h + 8 * g + i
+            turned = pltpu.roll(coefv[:, 128 * h : 128 * h + 128], lax.rem(128 - 32 * g, 128), 1)
+            for i in range(32):
+                l = 128 * h + 32 * g + i
                 pick = lambda k: jnp.broadcast_to(turned[8 * k : 8 * k + 8, i : i + 1], (8, 128))
                 choose = lambda k: jnp.where(
                     order_of_lane < 2,
@@ -211,18 +210,19 @@
 
         if h == 0:
             carry = (jnp.zeros((16, 128), F32),) * 4
-        carry = lax.fori_loop(0, 16 if h == 0 else 8, degrees, carry)
+        carry = lax.fori_loop(0, 4 if h == 0 else 2, degrees, carry)
 
     def finish(v, _):
         rows = pl.ds(pl.multiple_of((4 * (v // GROUPS) + lax.rem(v, GROUPS)) * NLAT, NLAT), NLAT)
         for u, store in ((0, legendre0), (1, legendre1)):
             part = store[rows, :].astype(BF16)
             table[v, :, 128 * u : 128 * u + 128] = part
-            table_t[v, 128 * u : 128 * u + 128, :] = part.T
         return 0
 
     lax.fori_loop(0, Q * GROUPS, finish, 0)
 
+    for load in loads[5:]:
+        load.wait()
     weights = weightv[...].T
     rotated[0] = jnp.where(low, weights, half(weights))
     rotated[1] = jnp.where(low, -half(weights), weights)
@@ -232,10 +232,10 @@
 
     order_of_row = lax.broadcasted_iota(jnp.int32, (256, 128), 0) % 16 // 4
     upper = lax.broadcasted_iota(jnp.int32, (1, 8, 128), 1) < 4
-    tile = lambda g: pl.ds(pl.multiple_of(g * 16, 16), 16)
+    tile = lambda g: pl.ds(g * 16, 16)
 
     def analyse(phase, q, into):
-        arrivals(phase, q)
+        whole(phase, q).wait_recv()
 
         def one(g, _):
             block = recv[phase, q, :, tile(g), :].reshape(256, 128)
@@ -244,7 +244,8 @@
             into[g] = into[g] + jnp.dot(table[GROUPS * q + g], spread, preferred_element_type=F32)
             return 0
 
-        lax.fori_loop(0, GROUPS, one, 0)
+        for g in range(GROUPS):
+            one(g, 0)
         return 0
 
     def synthesize(phase, q, scaled):
@@ -259,11 +260,25 @@
             send[phase, q, :, tile(g), :] = out.astype(BF16)
             return 0
 
-        lax.fori_loop(0, GROUPS, one, 0)
+        for g in range(GROUPS):
+            one(g, 0)
         ship(phase, q)
         return 0
 
-    lax.fori_loop(0, Q, lambda q, _: analyse(0, q, coeffs), 0)
+    def turn_table(v, _):
+        table_t[v] = table[v].T
+        return 0
+
+    def forward_chunk(q, _):
+        analyse(0, q, coeffs)
+
+        @pl.when(q == 1)
+        def _():
+            lax.fori_loop(0, Q * GROUPS, turn_table, 0)
+
+        return 0
+
+    lax.fori_loop(0, Q, forward_chunk, 0)
 
     def filter_group(g, _):
         for k in range(4):
@@ -272,11 +287,12 @@
             filtered[g, :, cols] = (rotated[0] * value + rotated[1] * half(value)).astype(BF16)
         return 0
 
-    lax.fori_loop(0, GROUPS, filter_group, 0)
+    for g in range(GROUPS):
+        filter_group(g, 0)
     lax.fori_loop(0, Q, lambda q, _: synthesize(1, q, False), 0)
 
     def gather(phase, q):
-        arrivals(phase, q)
+        whole(phase, q).wait_recv()
         stage[...] = recv[phase, q].reshape(N * PART, 128).astype(F32)
         for r in range(4):
             turned = stage[pl.ds(r, NLAT, stride=4), :].astype(BF16).T
@@ -322,7 +338,8 @@
             filtered[g, :, cols] = (rotated[0] * value - rotated[1] * half(value)).astype(BF16)
         return 0
 
-    lax.fori_loop(0, GROUPS, adjoint_group, 0)
+    for g in range(GROUPS):
+        adjoint_group(g, 0)
     synthesize(3, 0, True)
 
     def sum_group(g, _):
@@ -342,29 +359,26 @@
     def small_copy(turn, peer):
         return pltpu.make_async_remote_copy(
             src_ref=gout if turn else gsend.at[peer], dst_ref=(gall if turn else grecv).at[me],
-            send_sem=send_r.at[turn, peer], recv_sem=recv_r.at[turn, me],
+            send_sem=send_r.at[turn], recv_sem=recv_r.at[turn],
             device_id=(dp, peer), device_id_type=MESH,
         )
 
-    def small_arrivals(turn):
-        def arrival(src):
-            ref = (gall if turn else grecv).at[src]
-            pltpu.make_async_remote_copy(
-                src_ref=ref, dst_ref=ref, send_sem=send_r.at[turn, src], recv_sem=recv_r.at[turn, src],
-                device_id=(dp, src), device_id_type=MESH,
-            ).wait_recv()
-
-        each_peer(arrival)
+    def small_whole(turn):
+        ref = (gall if turn else grecv).at[pl.ds(0, N - 1)]
+        return pltpu.make_async_remote_copy(
+            src_ref=gsend.at[pl.ds(0, N - 1)], dst_ref=ref, send_sem=send_r.at[turn], recv_sem=recv_r.at[turn],
+            device_id=(dp, peer_of(1)), device_id_type=MESH,
+        )
 
     each_peer(lambda peer: small_copy(0, peer).start())
     grecv[me] = gsend[me]
-    lax.fori_loop(1, Q, lambda q, _: synthesize(3, q, True), 0)
-
-    small_arrivals(0)
+    synthesize(3, 1, True)
+    small_whole(0).wait_recv()
     total = (jnp.sum(grecv[...].astype(F32), axis=0) * (1.0 / NLAT)).astype(BF16)
     gout[...] = total
     gall[me] = total
     each_peer(lambda peer: small_copy(1, peer).start())
+    synthesize(3, 2, True)
 
     def gf_store(q):
         return pltpu.make_async_copy(xv.at[quad(q)], gf_hbm.at[quad(q)], store_sem.at[3 + q])
@@ -377,33 +391,35 @@
 
     lax.fori_loop(0, Q, gradient, 0)
 
-    small_arrivals(1)
+    small_whole(1).wait_recv()
     gwv[...] = gall[:ROWS].reshape(NLAT, 128).astype(F32).T
     gw_store = pltpu.make_async_copy(gwv, gw_hbm, store_sem.at[6])
     gw_store.start()
 
-    def drain(s, _):
-        peer = peer_of(s)
-        for phase in range(4):
-            for q in range(Q):
-                outgoing(phase, q, peer).wait_send()
-        for turn in range(2):
-            small_copy(turn, peer).wait_send()
-        return 0
-
-    lax.fori_loop(1, N, drain, 0)
+    for phase in range(4):
+        for q in range(Q):
+            whole(phase, q).wait_send()
+    for turn in range(2):
+        small_whole(turn).wait_send()
     for q in range(Q):
         act_store(q).wait()
         gf_store(q).wait()
     gw_store.wait()
 
 
-def hand_over(*refs):
-    count = (len(refs) - 1) // 2
-    copies = [pltpu.make_async_copy(refs[i], refs[count + i], refs[-1].at[i]) for i in range(count)]
-    for copy in copies:
+def hand_over(act, gf, gw, act_out, gf_out, gw_out, act_v, gf_v, gw_v, sems):
+    moves = [(gw, gw_v, gw_out)]
+    for q in range(Q):
+        rows = pl.ds(256 * q, 256)
+        moves += [(src.at[rows], mid.at[rows], dst.at[rows]) for src, mid, dst in ((act, act_v, act_out), (gf, gf_v, gf_out))]
+    ins = [pltpu.make_async_copy(src, mid, sems.at[0, i]) for i, (src, mid, _) in enumerate(moves)]
+    outs = [pltpu.make_async_copy(mid, dst, sems.at[1, i]) for i, (_, mid, dst) in enumerate(moves)]
+    for copy in ins:
         copy.start()
-    for copy in copies:
+    for before, after in zip(ins, outs):
+        before.wait()
+        after.start()
+    for copy in outs:
         copy.wait()
 
 
@@ -437,7 +453,7 @@
             vmem((2, 256, NLAT), BF16), vmem((flat, nlon), BF16), vmem((flat, nlon), BF16),
             vmem((N, 16, 128), BF16), vmem((N, 16, 128), BF16), vmem((16, 128), BF16), vmem((N, 16, 128), BF16),
             vmem((2, NLAT, 128), F32), vmem((2 * width, NLAT), F32),
-            dma((12,)), dma((7,)), dma((4, Q, N)), dma((4, Q, N)), dma((2, N)), dma((2, N)),
+            dma((12,)), dma((7,)), dma((4, Q)), dma((4, Q)), dma((2,)), dma((2,)),
         ],
         compiler_params=pltpu.CompilerParams(
             collective_id=0, has_side_effects=True, vmem_limit_bytes=56 << 20
@@ -451,7 +467,9 @@
         out_shape=shapes,
         in_specs=[pl.BlockSpec(memory_space=pl.ANY)] * 3,
         out_specs=(pl.BlockSpec(memory_space=pl.ANY),) * 3,
-        scratch_shapes=[dma((3,))],
+        scratch_shapes=[
+            vmem((flat, nlon), BF16), vmem((flat, nlon), BF16), vmem((2 * width, NLAT), F32), dma((2, 2 * Q + 1)),
+        ],
     )(*results)
     return (
         activated.reshape(rows, width, nlon), grad_fields.reshape(rows, width, nlon),

time: 131 us -> 49.7 us (0.38)
  Pallas kernels: 130 us -> 48.9 us
    pallas_call x1, Pallas kernels: 76.6 us -> 2.58 us  [shards(): pl.pallas_call(hand_over, out_shape=shapes, in_specs=[pl.BlockSpec(memory...]
    pallas_call x1, Pallas kernels: 53.5 us -> 46.3 us  [shards(): pl.pallas_call(kernel, out_shape=shapes, in_specs=[pl.BlockSpec(memory_sp...]
where the time goes in v3:
time: 49.7 us; the launch traced here: 49.5 us
  Pallas kernels  48.9 us (98%)
  between operations  0.64 us (1%)
    pallas_call x1, Pallas kernels, shards(): pl.pallas_call(kernel, out_shape=shapes, in_specs=[pl.BlockSpec(memory_sp...  46.3 us
    pallas_call x1, Pallas kernels, shards(): pl.pallas_call(hand_over, out_shape=shapes, in_specs=[pl.BlockSpec(memory...  2.58 us

profile of v3, /device:TPU:160, one launch (start us, length us, event | category | flops | bytes accessed | tf_op | source)
XLA Modules:
  0.0 49.5 jit_solution(3283032402880444808)
XLA Ops:
  0.6 46.3 %shard_map.121 = (bf16[768,768]{1,0:T(8,128)(2,1)}, bf16[768,768]{1,0:T(8,128)(2,1)}, f32[128,192]{1,0:T(8,128)}) custom-call(bf16[768,768]{1,0:T(8,128)(2,1)} %bitcast.6, bf16[768,768]{1,0:T(8,128)(2,1)} %bitcast.7, f32[128,192]{1,0:T(8,128)} %bitcast.8, bf16[384,768]{1,0:T(8,128)(2,1)} %constant.14.clone.ft_hbm, bf16[384,768]{1,0:T(8,128)(2,1)} %constant.15.clone.gt_hbm, ...), custom_call_target="tpu_custom_call" | custom-call | tf_op jit(solution)/shard_map/pallas_call | solution.py:439
  46.9 2.6 %shard_map.122 = (bf16[768,768]{1,0:T(8,128)(2,1)}, bf16[768,768]{1,0:T(8,128)(2,1)}, f32[128,192]{1,0:T(8,128)}) custom-call(bf16[768,768]{1,0:T(8,128)(2,1)} %get-tuple-element.9.act, bf16[768,768]{1,0:T(8,128)(2,1)} %get-tuple-element.10.gf, f32[128,192]{1,0:T(8,128)} %get-tuple-element.11.gw), custom_call_target="tpu_custom_call" | custom-call | tf_op jit(solution)/shard_map/pallas_call | solution.py:465

commit v4 on v3

--- a/solution.py
+++ b/solution.py
@@ -84,11 +84,11 @@
 
 def kernel(
     x_hbm, cot_hbm, weight_hbm, ft_hbm, gt_hbm, roww_hbm, colw_hbm, maps_hbm, diag_hbm, coef_hbm,
-    act_hbm, gf_hbm, gw_hbm,
+    act_ref, gf_ref, gw_ref,
     xv, cotv, weightv, ftv, gtv, rowwv, colwv, mapsv, diagv, coefv,
-    stage, send, recv, legendre0, legendre1, table, table_t, coeffs, dcoeffs, filtered, rotated, prev, tt, actv,
-    dprev, gsend, grecv, gout, gall, sums, gwv,
-    load_sem, store_sem, send_a, recv_a, send_r, recv_r,
+    stage, send, recv, legendre0, legendre1, table, table_t, coeffs, dcoeffs, filtered, rotated, prev, tt, dprev,
+    gsend, grecv, gout, gall, sums,
+    load_sem, send_a, recv_a, send_r, recv_r,
 ):
     dp, me = lax.axis_index("dp"), lax.axis_index("spatial")
     mx, my = me // 4, lax.rem(me, 4)
@@ -304,9 +304,6 @@
             tt[1], factors[NLAT:, :], preferred_element_type=F32
         )
 
-    def act_store(q):
-        return pltpu.make_async_copy(actv.at[quad(q)], act_hbm.at[quad(q)], store_sem.at[q])
-
     def activation(q, _):
         gather(1, q)
         prev[...] = grid_rows(gtv)
@@ -317,30 +314,18 @@
             pre = prev[here, :]
             cdf = 0.5 + 0.5 * lax.erf(pre * (1.0 / math.sqrt(2.0)))
             density = jnp.exp(-0.5 * pre * pre) * (1.0 / math.sqrt(2.0 * math.pi))
-            actv[there, :] = (pre * cdf).astype(BF16)
+            act_ref[there, :] = (pre * cdf).astype(BF16)
             dprev[there, :] = (cotv[there, :].astype(F32) * (cdf + pre * density)).astype(BF16)
             return 0
 
         lax.fori_loop(0, 16, strip, 0)
         fourier(2, q, dprev, gtv, False)
         ship(2, q)
-        act_store(q).start()
         return 0
 
     lax.fori_loop(0, Q, activation, 0)
 
     lax.fori_loop(0, Q, lambda q, _: analyse(2, q, dcoeffs), 0)
-
-    def adjoint_group(g, _):
-        for k in range(4):
-            cols = slice(128 * k, 128 * k + 128)
-            value = dcoeffs[g, :, cols]
-            filtered[g, :, cols] = (rotated[0] * value - rotated[1] * half(value)).astype(BF16)
-        return 0
-
-    for g in range(GROUPS):
-        adjoint_group(g, 0)
-    synthesize(3, 0, True)
 
     def sum_group(g, _):
         for k in range(4):
@@ -372,54 +357,48 @@
 
     each_peer(lambda peer: small_copy(0, peer).start())
     grecv[me] = gsend[me]
+    def adjoint_group(g, _):
+        for k in range(4):
+            cols = slice(128 * k, 128 * k + 128)
+            value = dcoeffs[g, :, cols]
+            filtered[g, :, cols] = (rotated[0] * value - rotated[1] * half(value)).astype(BF16)
+        return 0
+
+    for g in range(GROUPS):
+        adjoint_group(g, 0)
+    synthesize(3, 0, True)
+
     synthesize(3, 1, True)
+    synthesize(3, 2, True)
     small_whole(0).wait_recv()
     total = (jnp.sum(grecv[...].astype(F32), axis=0) * (1.0 / NLAT)).astype(BF16)
     gout[...] = total
     gall[me] = total
     each_peer(lambda peer: small_copy(1, peer).start())
-    synthesize(3, 2, True)
-
-    def gf_store(q):
-        return pltpu.make_async_copy(xv.at[quad(q)], gf_hbm.at[quad(q)], store_sem.at[3 + q])
 
     def gradient(q, _):
         gather(3, q)
-        xv[quad(q), :] = grid_rows(ftv).astype(BF16)
-        gf_store(q).start()
+        gf_ref[quad(q), :] = grid_rows(ftv).astype(BF16)
         return 0
 
     lax.fori_loop(0, Q, gradient, 0)
 
     small_whole(1).wait_recv()
-    gwv[...] = gall[:ROWS].reshape(NLAT, 128).astype(F32).T
-    gw_store = pltpu.make_async_copy(gwv, gw_hbm, store_sem.at[6])
-    gw_store.start()
+    gw_ref[...] = gall[:ROWS].reshape(NLAT, 128).astype(F32).T
 
     for phase in range(4):
         for q in range(Q):
             whole(phase, q).wait_send()
     for turn in range(2):
         small_whole(turn).wait_send()
-    for q in range(Q):
-        act_store(q).wait()
-        gf_store(q).wait()
-    gw_store.wait()
-
-
-def hand_over(act, gf, gw, act_out, gf_out, gw_out, act_v, gf_v, gw_v, sems):
-    moves = [(gw, gw_v, gw_out)]
-    for q in range(Q):
-        rows = pl.ds(256 * q, 256)
-        moves += [(src.at[rows], mid.at[rows], dst.at[rows]) for src, mid, dst in ((act, act_v, act_out), (gf, gf_v, gf_out))]
-    ins = [pltpu.make_async_copy(src, mid, sems.at[0, i]) for i, (src, mid, _) in enumerate(moves)]
-    outs = [pltpu.make_async_copy(mid, dst, sems.at[1, i]) for i, (_, mid, dst) in enumerate(moves)]
-    for copy in ins:
+
+
+def hand_over(act, gf, gw, act_out, gf_out, gw_out, sems):
+    moves = ((act, act_out), (gf, gf_out), (gw, gw_out))
+    copies = [pltpu.make_async_copy(src, dst, sems.at[i]) for i, (src, dst) in enumerate(moves)]
+    for copy in copies:
         copy.start()
-    for before, after in zip(ins, outs):
-        before.wait()
-        after.start()
-    for copy in outs:
+    for copy in copies:
         copy.wait()
 
 
@@ -438,9 +417,9 @@
     )
     results = pl.pallas_call(
         kernel,
-        out_shape=shapes,
+        out_shape=tuple(vmem(shape.shape, shape.dtype) for shape in shapes),
         in_specs=[pl.BlockSpec(memory_space=pl.ANY)] * 10,
-        out_specs=(pl.BlockSpec(memory_space=pl.ANY),) * 3,
+        out_specs=(pl.BlockSpec(memory_space=pltpu.VMEM),) * 3,
         scratch_shapes=[
             vmem((flat, nlon), BF16), vmem((flat, nlon), BF16), vmem((2 * width, NLAT), F32),
             vmem((2 * NLAT, nlon), BF16), vmem((2 * NLAT, nlon), BF16), vmem((16, 128), F32),
@@ -450,10 +429,10 @@
             vmem((Q * GROUPS, NLAT, 256), BF16), vmem((Q * GROUPS, 256, NLAT), BF16),
             vmem((GROUPS, NLAT, 512), F32), vmem((GROUPS, NLAT, 512), F32), vmem((GROUPS, NLAT, 512), BF16),
             vmem((2, NLAT, 128), F32), vmem((256, nlon), F32),
-            vmem((2, 256, NLAT), BF16), vmem((flat, nlon), BF16), vmem((flat, nlon), BF16),
+            vmem((2, 256, NLAT), BF16), vmem((flat, nlon), BF16),
             vmem((N, 16, 128), BF16), vmem((N, 16, 128), BF16), vmem((16, 128), BF16), vmem((N, 16, 128), BF16),
-            vmem((2, NLAT, 128), F32), vmem((2 * width, NLAT), F32),
-            dma((12,)), dma((7,)), dma((4, Q)), dma((4, Q)), dma((2,)), dma((2,)),
+            vmem((2, NLAT, 128), F32),
+            dma((12,)), dma((4, Q)), dma((4, Q)), dma((2,)), dma((2,)),
         ],
         compiler_params=pltpu.CompilerParams(
             collective_id=0, has_side_effects=True, vmem_limit_bytes=56 << 20
@@ -465,12 +444,10 @@
     activated, grad_fields, grad_weight = pl.pallas_call(
         hand_over,
         out_shape=shapes,
-        in_specs=[pl.BlockSpec(memory_space=pl.ANY)] * 3,
+        in_specs=[pl.BlockSpec(memory_space=pltpu.VMEM)] * 3,
         out_specs=(pl.BlockSpec(memory_space=pl.ANY),) * 3,
-        scratch_shapes=[
-            vmem((flat, nlon), BF16), vmem((flat, nlon), BF16), vmem((2 * width, NLAT), F32), dma((2, 2 * Q + 1)),
-        ],
-    )(*results)
+        scratch_shapes=[dma((3,))],
+    )(*(pltpu.with_memory_space_constraint(result, pltpu.VMEM) for result in results))
     return (
         activated.reshape(rows, width, nlon), grad_fields.reshape(rows, width, nlon),
         grad_weight.reshape(2, width, NLAT),

time: 49.7 us -> 45.6 us (0.918)
  Pallas kernels: 48.9 us -> 44.9 us
    pallas_call x1, Pallas kernels: 46.3 us -> 43.4 us  [shards(): pl.pallas_call(kernel, out_shape=tuple((vmem(shape.shape, shape.dtype) fo...]
    pallas_call x1, Pallas kernels: 2.58 us -> 1.46 us  [shards(): pl.pallas_call(hand_over, out_shape=shapes, in_specs=[pl.BlockSpec(memory...]
where the time goes in v4:
time: 45.6 us; the launch traced here: 45.5 us
  Pallas kernels  44.9 us (98%)
  between operations  0.64 us (1%)
    pallas_call x1, Pallas kernels, shards(): pl.pallas_call(kernel, out_shape=tuple((vmem(shape.shape, shape.dtype) fo...  43.4 us
    pallas_call x1, Pallas kernels, shards(): pl.pallas_call(hand_over, out_shape=shapes, in_specs=[pl.BlockSpec(memory...  1.46 us

profile of v4, /device:TPU:160, one launch (start us, length us, event | category | flops | bytes accessed | tf_op | source)
XLA Modules:
  0.0 45.5 jit_solution(17212650861378072968)
XLA Ops:
  0.6 43.4 %shard_map.121 = (bf16[768,768]{1,0:T(8,128)(2,1)S(1)}, bf16[768,768]{1,0:T(8,128)(2,1)S(1)}, f32[128,192]{1,0:T(8,128)S(1)}) custom-call(bf16[768,768]{1,0:T(8,128)(2,1)} %bitcast.6, bf16[768,768]{1,0:T(8,128)(2,1)} %bitcast.7, f32[128,192]{1,0:T(8,128)} %bitcast.8, bf16[384,768]{1,0:T(8,128)(2,1)} %constant.14.clone.ft_hbm, ...), custom_call_target="tpu_custom_call" | custom-call | tf_op jit(solution)/shard_map/pallas_call | solution.py:418
  44.1 1.5 %shard_map.122 = (bf16[768,768]{1,0:T(8,128)(2,1)}, bf16[768,768]{1,0:T(8,128)(2,1)}, f32[128,192]{1,0:T(8,128)}) custom-call(bf16[768,768]{1,0:T(8,128)(2,1)S(1)} %get-tuple-element.9.act, bf16[768,768]{1,0:T(8,128)(2,1)S(1)} %get-tuple-element.10.gf, f32[128,192]{1,0:T(8,128)S(1)} %get-tuple-element.11.gw), custom_call_target="tpu_custom_call" | custom-call | tf_op jit(solution)/shard_map/pallas_call | solution.py:444

commit v5 on v4

--- a/solution.py
+++ b/solution.py
@@ -87,24 +87,17 @@
     act_ref, gf_ref, gw_ref,
     xv, cotv, weightv, ftv, gtv, rowwv, colwv, mapsv, diagv, coefv,
     stage, send, recv, legendre0, legendre1, table, table_t, coeffs, dcoeffs, filtered, rotated, prev, tt, dprev,
-    gsend, grecv, gout, gall, sums,
+    gsend, grecv, gout, gall,
     load_sem, send_a, recv_a, send_r, recv_r,
 ):
     dp, me = lax.axis_index("dp"), lax.axis_index("spatial")
     mx, my = me // 4, lax.rem(me, 4)
     at = lambda dx, dy: lax.rem(mx + dx, 4) * 4 + lax.rem(my + dy, 4)
-    peer_of = lambda s: lax.rem(me + s, N)
-
-    def each_peer(action):
-        def one(s, _):
-            action(peer_of(s))
-            return 0
-
-        lax.fori_loop(1, N, one, 0)
+    peers = [at(dx, dy) for dx, dy in OFFSETS]
 
     barrier = pltpu.get_barrier_semaphore()
-    for dx, dy in OFFSETS:
-        pl.semaphore_signal(barrier, inc=1, device_id=(dp, at(dx, dy)), device_id_type=MESH)
+    for peer in peers:
+        pl.semaphore_signal(barrier, inc=1, device_id=(dp, peer), device_id_type=MESH)
 
     quad = lambda q: pl.ds(pl.multiple_of(q * 256, 256), 256)
 
@@ -141,12 +134,12 @@
         return pltpu.make_async_remote_copy(
             src_ref=send.at[phase, q, pl.ds(0, N - 1)], dst_ref=recv.at[phase, q, pl.ds(0, N - 1)],
             send_sem=send_a.at[phase, q], recv_sem=recv_a.at[phase, q],
-            device_id=(dp, peer_of(1)), device_id_type=MESH,
+            device_id=(dp, peers[0]), device_id_type=MESH,
         )
 
     def ship(phase, q):
-        for dx, dy in OFFSETS:
-            outgoing(phase, q, at(dx, dy)).start()
+        for peer in peers:
+            outgoing(phase, q, peer).start()
         recv[phase, q, me] = send[phase, q, me]
 
     def fourier(phase, q, rows_ref, factors, scaled):
@@ -228,7 +221,6 @@
     rotated[1] = jnp.where(low, -half(weights), weights)
     coeffs[...] = jnp.zeros_like(coeffs)
     dcoeffs[...] = jnp.zeros_like(dcoeffs)
-    sums[...] = jnp.zeros_like(sums)
 
     order_of_row = lax.broadcasted_iota(jnp.int32, (256, 128), 0) % 16 // 4
     upper = lax.broadcasted_iota(jnp.int32, (1, 8, 128), 1) < 4
@@ -327,16 +319,9 @@
 
     lax.fori_loop(0, Q, lambda q, _: analyse(2, q, dcoeffs), 0)
 
-    def sum_group(g, _):
-        for k in range(4):
-            cols = slice(128 * k, 128 * k + 128)
-            value, coeff = dcoeffs[g, :, cols], coeffs[g, :, cols]
-            sums[0] = sums[0] + value * coeff
-            sums[1] = sums[1] + value * half(coeff)
-        return 0
-
-    lax.fori_loop(0, GROUPS, sum_group, 0)
-    same, cross = sums[0], sums[1]
+    places = [(g, slice(None), slice(128 * k, 128 * k + 128)) for g in range(GROUPS) for k in range(4)]
+    same = sum(dcoeffs[place] * coeffs[place] for place in places)
+    cross = sum(dcoeffs[place] * half(coeffs[place]) for place in places)
     partial = jnp.where(low, same + half(same), cross - half(cross)).astype(BF16)
     gsend[:ROWS] = partial.reshape(ROWS, 16, 128)
     gsend[ROWS:] = jnp.zeros((N - ROWS, 16, 128), BF16)
@@ -352,10 +337,11 @@
         ref = (gall if turn else grecv).at[pl.ds(0, N - 1)]
         return pltpu.make_async_remote_copy(
             src_ref=gsend.at[pl.ds(0, N - 1)], dst_ref=ref, send_sem=send_r.at[turn], recv_sem=recv_r.at[turn],
-            device_id=(dp, peer_of(1)), device_id_type=MESH,
+            device_id=(dp, peers[0]), device_id_type=MESH,
         )
 
-    each_peer(lambda peer: small_copy(0, peer).start())
+    for peer in peers:
+        small_copy(0, peer).start()
     grecv[me] = gsend[me]
     def adjoint_group(g, _):
         for k in range(4):
@@ -374,7 +360,8 @@
     total = (jnp.sum(grecv[...].astype(F32), axis=0) * (1.0 / NLAT)).astype(BF16)
     gout[...] = total
     gall[me] = total
-    each_peer(lambda peer: small_copy(1, peer).start())
+    for peer in peers:
+        small_copy(1, peer).start()
 
     def gradient(q, _):
         gather(3, q)
@@ -431,7 +418,6 @@
             vmem((2, NLAT, 128), F32), vmem((256, nlon), F32),
             vmem((2, 256, NLAT), BF16), vmem((flat, nlon), BF16),
             vmem((N, 16, 128), BF16), vmem((N, 16, 128), BF16), vmem((16, 128), BF16), vmem((N, 16, 128), BF16),
-            vmem((2, NLAT, 128), F32),
             dma((12,)), dma((4, Q)), dma((4, Q)), dma((2,)), dma((2,)),
         ],
         compiler_params=pltpu.CompilerParams(

time: 45.6 us -> 44.7 us (0.980)
  Pallas kernels: 44.9 us -> 44 us
    pallas_call x1, Pallas kernels: 43.4 us -> 42.5 us  [shards(): pl.pallas_call(kernel, out_shape=tuple((vmem(shape.shape, shape.dtype) fo...]
where the time goes in v5:
time: 44.7 us; the launch traced here: 44.6 us
  Pallas kernels  44 us (98%)
  between operations  0.64 us (1%)
    pallas_call x1, Pallas kernels, shards(): pl.pallas_call(kernel, out_shape=tuple((vmem(shape.shape, shape.dtype) fo...  42.5 us
    pallas_call x1, Pallas kernels, shards(): pl.pallas_call(hand_over, out_shape=shapes, in_specs=[pl.BlockSpec(memory...  1.46 us

profile of v5, /device:TPU:160, one launch (start us, length us, event | category | flops | bytes accessed | tf_op | source)
XLA Modules:
  0.0 44.6 jit_solution(7892471780584795579)
XLA Ops:
  0.6 42.5 %shard_map.121 = (bf16[768,768]{1,0:T(8,128)(2,1)S(1)}, bf16[768,768]{1,0:T(8,128)(2,1)S(1)}, f32[128,192]{1,0:T(8,128)S(1)}) custom-call(bf16[768,768]{1,0:T(8,128)(2,1)} %bitcast.6, bf16[768,768]{1,0:T(8,128)(2,1)} %bitcast.7, f32[128,192]{1,0:T(8,128)} %bitcast.8, bf16[384,768]{1,0:T(8,128)(2,1)} %constant.14.clone.ft_hbm, ...), custom_call_target="tpu_custom_call" | custom-call | tf_op jit(solution)/shard_map/pallas_call | solution.py:405
  43.2 1.5 %shard_map.122 = (bf16[768,768]{1,0:T(8,128)(2,1)}, bf16[768,768]{1,0:T(8,128)(2,1)}, f32[128,192]{1,0:T(8,128)}) custom-call(bf16[768,768]{1,0:T(8,128)(2,1)S(1)} %get-tuple-element.9.act, bf16[768,768]{1,0:T(8,128)(2,1)S(1)} %get-tuple-element.10.gf, f32[128,192]{1,0:T(8,128)S(1)} %get-tuple-element.11.gw), custom_call_target="tpu_custom_call" | custom-call | tf_op jit(solution)/shard_map/pallas_call | solution.py:430

commit v6 on v5

--- a/solution.py
+++ b/solution.py
@@ -86,7 +86,7 @@
     x_hbm, cot_hbm, weight_hbm, ft_hbm, gt_hbm, roww_hbm, colw_hbm, maps_hbm, diag_hbm, coef_hbm,
     act_ref, gf_ref, gw_ref,
     xv, cotv, weightv, ftv, gtv, rowwv, colwv, mapsv, diagv, coefv,
-    stage, send, recv, legendre0, legendre1, table, table_t, coeffs, dcoeffs, filtered, rotated, prev, tt, dprev,
+    stage, send, recv, legendre0, legendre1, table, table_t, coeffs, turned, dcoeffs, filtered, rotated, prev, tt, dprev,
     gsend, grecv, gout, gall,
     load_sem, send_a, recv_a, send_r, recv_r,
 ):
@@ -282,6 +282,9 @@
     for g in range(GROUPS):
         filter_group(g, 0)
     lax.fori_loop(0, Q, lambda q, _: synthesize(1, q, False), 0)
+    for g in range(GROUPS):
+        for k in range(4):
+            turned[g, :, 128 * k : 128 * k + 128] = half(coeffs[g, :, 128 * k : 128 * k + 128])
 
     def gather(phase, q):
         whole(phase, q).wait_recv()
@@ -321,7 +324,7 @@
 
     places = [(g, slice(None), slice(128 * k, 128 * k + 128)) for g in range(GROUPS) for k in range(4)]
     same = sum(dcoeffs[place] * coeffs[place] for place in places)
-    cross = sum(dcoeffs[place] * half(coeffs[place]) for place in places)
+    cross = sum(dcoeffs[place] * turned[place] for place in places)
     partial = jnp.where(low, same + half(same), cross - half(cross)).astype(BF16)
     gsend[:ROWS] = partial.reshape(ROWS, 16, 128)
     gsend[ROWS:] = jnp.zeros((N - ROWS, 16, 128), BF16)
@@ -414,7 +417,7 @@
             vmem((N * PART, 128), F32), vmem((4, Q, N, PART, 128), BF16), vmem((4, Q, N, PART, 128), BF16),
             vmem((16 * NLAT, 128), F32), vmem((16 * NLAT, 128), F32),
             vmem((Q * GROUPS, NLAT, 256), BF16), vmem((Q * GROUPS, 256, NLAT), BF16),
-            vmem((GROUPS, NLAT, 512), F32), vmem((GROUPS, NLAT, 512), F32), vmem((GROUPS, NLAT, 512), BF16),
+            vmem((GROUPS, NLAT, 512), F32), vmem((GROUPS, NLAT, 512), F32), vmem((GROUPS, NLAT, 512), F32), vmem((GROUPS, NLAT, 512), BF16),
             vmem((2, NLAT, 128), F32), vmem((256, nlon), F32),
             vmem((2, 256, NLAT), BF16), vmem((flat, nlon), BF16),
             vmem((N, 16, 128), BF16), vmem((N, 16, 128), BF16), vmem((16, 128), BF16), vmem((N, 16, 128), BF16),

time: 44.7 us -> 44.5 us (level)
  no operation moved by 1% of the time
where the time goes in v6:
time: 44.5 us; the launch traced here: 44.4 us
  Pallas kernels  43.7 us (98%)
  between operations  0.64 us (1%)
    pallas_call x1, Pallas kernels, shards(): pl.pallas_call(kernel, out_shape=tuple((vmem(shape.shape, shape.dtype) fo...  42.3 us
    pallas_call x1, Pallas kernels, shards(): pl.pallas_call(hand_over, out_shape=shapes, in_specs=[pl.BlockSpec(memory...  1.46 us

profile of v6, /device:TPU:160, one launch (start us, length us, event | category | flops | bytes accessed | tf_op | source)
XLA Modules:
  0.0 44.4 jit_solution(16417478366301631788)
XLA Ops:
  0.6 42.3 %shard_map.121 = (bf16[768,768]{1,0:T(8,128)(2,1)S(1)}, bf16[768,768]{1,0:T(8,128)(2,1)S(1)}, f32[128,192]{1,0:T(8,128)S(1)}) custom-call(bf16[768,768]{1,0:T(8,128)(2,1)} %bitcast.6, bf16[768,768]{1,0:T(8,128)(2,1)} %bitcast.7, f32[128,192]{1,0:T(8,128)} %bitcast.8, bf16[384,768]{1,0:T(8,128)(2,1)} %constant.14.clone.ft_hbm, ...), custom_call_target="tpu_custom_call" | custom-call | tf_op jit(solution)/shard_map/pallas_call | solution.py:408
  42.9 1.5 %shard_map.122 = (bf16[768,768]{1,0:T(8,128)(2,1)}, bf16[768,768]{1,0:T(8,128)(2,1)}, f32[128,192]{1,0:T(8,128)}) custom-call(bf16[768,768]{1,0:T(8,128)(2,1)S(1)} %get-tuple-element.9.act, bf16[768,768]{1,0:T(8,128)(2,1)S(1)} %get-tuple-element.10.gf, f32[128,192]{1,0:T(8,128)S(1)} %get-tuple-element.11.gw), custom_call_target="tpu_custom_call" | custom-call | tf_op jit(solution)/shard_map/pallas_call | solution.py:433
